TPU v7x, 256 devices: a whole 4x4x8 slice. The times are simulated.
256 devices in a mesh: dp: 8 (over y_lo, x), space: 32 (over z, y_hi, core).
Axes of the slice: x: 4, y: 4 (y_hi: 2, y_lo: 2; y = y_hi * 2 + y_lo), z: 8, core: 2. Of those that a mesh axis runs over, the one named last changes fastest.
Arguments:
- volumes: bfloat16 [8, 32, 64, 48, 128], P('dp', None, 'space'), may hold values from -6 to 6
- kernel: bfloat16 [3, 3, 3, 64, 32], replicated, may hold values from -0.21875 to 0.21875
- bias: float32 [64], replicated, may hold values from -3 to 3
- cotangent: bfloat16 [8, 64, 64, 48, 128], P('dp', None, 'space'), may hold values from -6 to 6
- finished_grads: float32 [8, 32, 262144], P('dp', 'space'), may hold values from -0.5 to 0.5
Outputs:
- activations: bfloat16 [8, 64, 64, 48, 128], P('dp', None, 'space')
- grad_volumes: bfloat16 [8, 32, 64, 48, 128], P('dp', None, 'space')
- grad_kernel: float32 [3, 3, 3, 64, 32], replicated
- grad_bias: float32 [64], replicated
- summed_grads: float32 [262144], replicated
All inputs are finite; a program needn't handle non-finite values.
Results may differ from a plain program's by a relative error of at most 0.006.
Values may be sent and summed in bfloat16 or wider, within the bound.
No kernel may reach another device: no remote copies, remote signals or barrier semaphores. Data moves between devices by JAX's collectives and lax.ppermute only.
A program may use at most 128 MiB of HBM per device.

v0:
```python
import math

import jax
import jax.numpy as jnp
from jax import lax
from jax.experimental import pallas as pl
from jax.experimental.pallas import tpu as pltpu
from jax.sharding import Mesh, PartitionSpec as P

BF = jnp.bfloat16
F32 = jnp.float32
CI, CO, NY, NX = 32, 64, 48, 128
PADY = NY + 2
PLANE = ("yl", "x", "yh", "c")
COLUMN = "z"
CHUNKS, COLS = 32, 8
FROWS, TROWS = 64, 16
SPACE = ("z", "yh", "c")


def call(body, outs, scratch, specs, flops, nbytes, out_specs=None):
    return pl.pallas_call(
        body,
        out_shape=outs,
        in_specs=specs,
        out_specs=out_specs or jax.tree.map(lambda _: VM, outs),
        scratch_shapes=scratch,
        compiler_params=pltpu.CompilerParams(vmem_limit_bytes=48 << 20),
        cost_estimate=pl.CostEstimate(flops=flops, transcendentals=0, bytes_accessed=nbytes),
    )


VM = pl.BlockSpec(memory_space=pltpu.VMEM)
HBM = pl.BlockSpec(memory_space=pltpu.HBM)
ANY = pl.BlockSpec(memory_space=pl.ANY)
DMA = pltpu.SemaphoreType.DMA


def turn_kernel(x_ref, p0_ref, p1_ref, x, s0, s1, b0, b1, in_sem, out_sem):
    parts = [
        pltpu.make_async_copy(x_ref.at[pl.ds(8 * n, 8)], x.at[pl.ds(8 * n, 8)], in_sem.at[n])
        for n in range(4)
    ]
    for part in parts:
        part.start()
    for b in (b0, b1):
        b[0:CI, :] = jnp.zeros((CI, NX), BF)
        b[CI * (NY + 1) : CI * PADY, :] = jnp.zeros((CI, NX), BF)
    for n, part in enumerate(parts):
        part.wait()
        for c in range(8 * n, 8 * n + 8):
            for z, s in ((0, s0), (1, s1)):
                s[pl.ds(c, NY, stride=CI), :] = x[c, z].astype(F32)
    outs = []
    for n, (p, s, b) in enumerate(((p0_ref, s0, b0), (p1_ref, s1, b1))):
        b[CI : CI * (NY + 1), :] = s[...].astype(BF)
        outs.append(pltpu.make_async_copy(b, p, out_sem.at[n]))
        outs[-1].start()
    for out in outs:
        out.wait()


def shifted_sum(before, middle, after):
    lane = lax.broadcasted_iota(jnp.int32, middle.shape, 1)
    left = jnp.where(lane == 0, 0.0, pltpu.roll(before, 1, 1))
    right = jnp.where(lane == NX - 1, 0.0, pltpu.roll(after, NX - 1, 1))
    return middle + left + right


HALF = NY // 2 + 2


def halves(planes, buffers, width, sems):
    first, second = [], []
    for n, (p, b) in enumerate(zip(planes, buffers)):
        for part, rows, at in ((first, pl.ds(0, HALF * width), 0), (second, pl.ds(HALF * width, (PADY - HALF) * width), 1)):
            part.append(pltpu.make_async_copy(p.at[rows], b.at[rows], sems.at[2 * n + at]))
    for copy in first + second:
        copy.start()
    return first, second


def forward_kernel(*refs):
    p_refs, (a_ref, bias_ref, cot_ref, act_ref, g0_ref, g1_ref) = refs[:4], refs[4:10]
    planes, (a, cot, act, g0, g1, s0, s1, in_sem, act_sem) = refs[10:14], refs[14:]
    a_copy = pltpu.make_async_copy(a_ref, a, in_sem.at[8])
    a_copy.start()
    first, second = halves(p_refs, planes, CI, in_sem)
    cot_copy = pltpu.make_async_copy(cot_ref, cot, in_sem.at[9])
    cot_copy.start()
    for g in (g0, g1):
        g[0:CO, :] = jnp.zeros((CO, NX), BF)
        g[CO * (NY + 1) : CO * PADY, :] = jnp.zeros((CO, NX), BF)

    def conv(q, _):
        sides = []
        for h in range(2):
            start = pl.multiple_of((2 * q + h) * (2 * CI), 2 * CI)
            sides.append(jnp.concatenate([p[pl.ds(start, 4 * CI), :] for p in planes], axis=0))
        rhs = jnp.concatenate(sides, axis=1)
        r = jnp.dot(a[...], rhs, preferred_element_type=F32)
        for h in range(2):
            rr = r[:, NX * h : NX * (h + 1)]
            y = shifted_sum(rr[0:256], rr[256:512], rr[512:768])
            at = pl.multiple_of((2 * q + h) * 128, 128)
            s0[pl.ds(at, 128), :] = y[0:128]
            s1[pl.ds(at, 128), :] = y[128:256]
        return 0

    a_copy.wait()
    for part, lo in ((first, 0), (second, 6)):
        for copy in part:
            copy.wait()
        lax.fori_loop(lo, lo + 6, conv, 0)
    cot_copy.wait()

    def point(o, _):
        b = bias_ref[o]
        for z, s in ((0, s0), (1, s1)):
            v = s[pl.ds(o, NY, stride=CO), :] + b
            sig = 0.5 + 0.5 * jnp.tanh(0.5 * jnp.abs(v))
            soft = jnp.maximum(v, 0.0) - jnp.log(sig)
            act[o, z] = (0.3 * v + 0.7 * soft).astype(BF)
            slope = 0.3 + 0.7 * jnp.where(v >= 0, sig, 1.0 - sig)
            s[pl.ds(o, NY, stride=CO), :] = cot[o, z].astype(F32) * slope
        return 0

    outs = []
    for n in range(4):
        lax.fori_loop(16 * n, 16 * n + 16, point, 0, unroll=2)
        some = pl.ds(16 * n, 16)
        outs.append(pltpu.make_async_copy(act.at[some], act_ref.at[some], act_sem.at[n]))
        outs[-1].start()
    for n, (g_ref, g, s) in enumerate(((g0_ref, g0, s0), (g1_ref, g1, s1))):
        g[CO : CO * (NY + 1), :] = s[...].astype(BF)
        outs.append(pltpu.make_async_copy(g, g_ref, act_sem.at[4 + n]))
        outs[-1].start()
    for out in outs:
        out.wait()


def weight_kernel(*refs):
    p_refs, g_refs, out_ref = refs[:4], refs[4:6], refs[6]
    planes, gs_buf, acc, sems = refs[7:11], refs[11:13], refs[13], refs[14]
    first, second = halves(p_refs, planes, CI, sems)
    g_first, g_second = halves(g_refs, gs_buf, CO, sems.at[pl.ds(8, 4)])
    acc[...] = jnp.zeros_like(acc)
    lane = lax.broadcasted_iota(jnp.int32, (CO, NX), 1)

    def row(y, _):
        gs, xs = [], []
        ystart = pl.multiple_of(y * CI, CI)
        gstart = pl.multiple_of((y + 1) * CO, CO)
        for z, g in enumerate(gs_buf):
            mid = g[pl.ds(gstart, CO), :]
            wide = mid.astype(F32)
            before = jnp.where(lane == NX - 1, 0.0, pltpu.roll(wide, NX - 1, 1)).astype(BF)
            after = jnp.where(lane == 0, 0.0, pltpu.roll(wide, 1, 1)).astype(BF)
            gs.append(jnp.concatenate([before, mid, after], axis=0))
            xs.append(
                jnp.concatenate(
                    [planes[z + i][pl.ds(ystart, 3 * CI), :] for i in range(3)]
                    + [jnp.ones((16, NX), BF)],
                    axis=0,
                )
            )
        acc[...] += lax.dot_general(
            jnp.concatenate(xs, axis=1),
            jnp.concatenate(gs, axis=1),
            (((1,), (1,)), ((), ())),
            preferred_element_type=F32,
        )
        return 0

    for part, lo in ((first + g_first, 0), (second + g_second, 24)):
        for copy in part:
            copy.wait()
        lax.fori_loop(lo, lo + 24, row, 0, unroll=2)
    out_ref[0:288, :] = acc[0:288, 0:128].astype(BF)
    side = acc[0:288, 128:192]
    tail = jnp.concatenate([side[160:288], jnp.zeros((32, CO), F32)], axis=0)
    out_ref[288:448, :] = jnp.concatenate([side[0:160], tail], axis=1).astype(BF)
    out_ref[448:464, :] = acc[288:304, 0:128].astype(BF)
    out_ref[464:512, :] = jnp.zeros((48, NX), BF)


def back_kernel(*refs):
    p_refs, d_ref, out_ref = refs[:4], refs[4], refs[5]
    planes, (d, buf, s0, s1, sems, out_sem) = refs[6:10], refs[10:]
    d_copy = pltpu.make_async_copy(d_ref, d, sems.at[8])
    d_copy.start()
    first, second = halves(p_refs, planes, CO, sems)

    def conv(q, _):
        for z, s in ((0, s0), (1, s1)):
            sides = []
            for h in range(2):
                start = pl.multiple_of((2 * q + h) * (2 * CO), 2 * CO)
                sides.append(
                    jnp.concatenate(
                        [planes[z + 2 - i][pl.ds(start, 4 * CO), :] for i in range(3)], axis=0
                    )
                )
            r = jnp.dot(d[...], jnp.concatenate(sides, axis=1), preferred_element_type=F32)
            for h in range(2):
                rr = r[:, NX * h : NX * (h + 1)]
                at = pl.multiple_of((2 * q + h) * (2 * CI), 2 * CI)
                s[pl.ds(at, 2 * CI), :] = shifted_sum(rr[128:192], rr[64:128], rr[0:64])
        return 0

    d_copy.wait()
    for part, lo in ((first, 0), (second, 6)):
        for copy in part:
            copy.wait()
        lax.fori_loop(lo, lo + 6, conv, 0)

    def gather(c, _):
        for z, s in ((0, s0), (1, s1)):
            buf[c, z] = s[pl.ds(c, NY, stride=CI), :].astype(BF)
        return 0

    outs = []
    for n in range(2):
        lax.fori_loop(16 * n, 16 * n + 16, gather, 0, unroll=4)
        some = pl.ds(16 * n, 16)
        outs.append(pltpu.make_async_copy(buf.at[some], out_ref.at[some], out_sem.at[n]))
        outs[-1].start()
    for out in outs:
        out.wait()


def prep_kernel(w_ref, f_ref, a_out, d_out, out_ref, turned, a_ref, d_ref, sem):
    out_ref[...] = f_ref[...].reshape(CHUNKS, FROWS, NX).astype(BF)
    for z, hole in ((0, 3), (1, 0)):
        for k in range(3):
            col = (k * 2 + z) * 128
            turned[hole * 128 : hole * 128 + 128, col : col + 128] = jnp.zeros((128, 128), F32)
    for i in range(3):
        for k in range(3):
            w = [w_ref[i, j, k].astype(F32) for j in range(3)]
            none = jnp.zeros((CI, CO), F32)
            for s in range(4):
                pair = jnp.concatenate([w[s] if s < 3 else none, w[s - 1] if s else none], axis=1)
                y, p = ((0, 1), (1, 1), (0, 0), (1, 0))[s]
                row, col = (k * 2 + y) * CI, i * 256 + p * 128
                d_ref[row : row + CI, col : col + 128] = pair.astype(BF)
                for z in range(2):
                    row, col = ((i + z) * 4 + s) * CI, (k * 2 + z) * 128
                    turned[row : row + CI, col : col + 128] = pair
    d_copy = pltpu.make_async_copy(d_ref, d_out, sem.at[0])
    d_copy.start()
    a_ref[...] = turned[...].T.astype(BF)
    a_copy = pltpu.make_async_copy(a_ref, a_out, sem.at[1])
    a_copy.start()
    d_copy.wait()
    a_copy.wait()


def join_b_kernel(f_ref, t_ref, out_ref):
    f = jnp.sum(f_ref[...].astype(F32), axis=0).astype(BF)
    t = jnp.sum(t_ref[...].astype(F32), axis=0).astype(BF)
    for n in range(COLS):
        out_ref[n, 0:FROWS] = f
        out_ref[n, FROWS:] = t


def join_c_kernel(in_ref, out_ref):
    both = jnp.sum(in_ref[...].astype(F32), axis=0).astype(BF)
    for n in range(CHUNKS):
        out_ref[n] = both


def out_kernel(in_ref, sum_ref, taps_ref, bias_ref):
    sum_ref[...] = in_ref[:, 0:FROWS, :].astype(F32).reshape(CHUNKS * FROWS, NX)
    scale = 1.0 / math.sqrt(8 * 64 * NY * NX)
    t = in_ref[:, FROWS:, :].astype(F32).reshape(CHUNKS * TROWS, NX) * scale
    for ij in range(9):
        two = t[ij * CI : ij * CI + CI]
        taps_ref[ij, 0] = two[:, 0:CO]
        taps_ref[ij, 1] = two[:, CO : 2 * CO]
        at, lane = (288 + ij * CI, 0) if ij < 5 else (288 + (ij - 5) * CI, CO)
        taps_ref[ij, 2] = t[at : at + CI, lane : lane + CO]
    bias_ref[...] = t[448:449, CO : 2 * CO]


def exchange(parts, axes):
    return lax.all_to_all(parts, axes, 0, 0)


def join_b(fin, taps):
    sds = jax.ShapeDtypeStruct((COLS, FROWS + TROWS, NX), BF)
    return call(join_b_kernel, sds, [], [VM] * 2, 1 << 20, 1 << 20)(fin, taps)


def join_c(parts):
    sds = jax.ShapeDtypeStruct((CHUNKS, FROWS + TROWS, NX), BF)
    return call(join_c_kernel, sds, [], [VM], 1 << 20, 1 << 20)(parts)


def neighbours(low, high):
    up = [(i, i + 1) for i in range(31)]
    down = [(i + 1, i) for i in range(31)]
    return lax.ppermute(high, SPACE, up), lax.ppermute(low, SPACE, down)


def far(x):
    return pltpu.with_memory_space_constraint(x, pltpu.HBM)


def layer(volumes, kernel, bias, cotangent, finished_grads):
    sds = jax.ShapeDtypeStruct
    x_plane = sds((PADY * CI, NX), BF)
    g_plane = sds((PADY * CO, NX), BF)
    turn = call(
        turn_kernel,
        (pltpu.HBM(x_plane.shape, BF), pltpu.HBM(x_plane.shape, BF)),
        [pltpu.VMEM((CI, 2, NY, NX), BF)]
        + [pltpu.VMEM((NY * CI, NX), F32)] * 2
        + [pltpu.VMEM((PADY * CI, NX), BF)] * 2
        + [DMA((4,)), DMA((2,))],
        [HBM],
        1 << 22,
        3 << 20,
        (HBM, HBM),
    )
    xbuf = pltpu.VMEM((PADY * CI, NX), BF)
    gbuf = pltpu.VMEM((PADY * CO, NX), BF)
    g_out = pltpu.HBM(g_plane.shape, BF)
    forward = call(
        forward_kernel,
        (pltpu.HBM((CO, 2, NY, NX), BF), g_out, g_out),
        [xbuf] * 4
        + [pltpu.VMEM((768, 512), BF)]
        + [pltpu.VMEM((CO, 2, NY, NX), BF)] * 2
        + [gbuf] * 2
        + [pltpu.VMEM((NY * CO, NX), F32)] * 2
        + [DMA((10,)), DMA((6,))],
        [ANY, HBM, HBM, ANY, HBM, pl.BlockSpec(memory_space=pltpu.SMEM), HBM],
        3 << 32,
        8 << 20,
        (HBM, HBM, HBM),
    )
    weight = call(
        weight_kernel,
        sds((512, NX), BF),
        [xbuf] * 4 + [gbuf] * 2 + [pltpu.VMEM((304, 192), F32), DMA((12,))],
        [ANY, HBM, HBM, ANY, HBM, HBM],
        3 << 32,
        5 << 20,
    )
    back = call(
        back_kernel,
        pltpu.HBM((CI, 2, NY, NX), BF),
        [gbuf] * 4
        + [pltpu.VMEM((192, 768), BF), pltpu.VMEM((CI, 2, NY, NX), BF)]
        + [pltpu.VMEM((NY * CI, NX), F32)] * 2
        + [DMA((9,)), DMA((2,))],
        [ANY, HBM, HBM, ANY, HBM],
        3 << 32,
        8 << 20,
        HBM,
    )
    prep = call(
        prep_kernel,
        (pltpu.HBM((768, 512), BF), pltpu.HBM((192, 768), BF), sds((CHUNKS, FROWS, NX), BF)),
        [
            pltpu.VMEM((512, 768), F32),
            pltpu.VMEM((768, 512), BF),
            pltpu.VMEM((192, 768), BF),
            DMA((2,)),
        ],
        [VM] * 2,
        1 << 22,
        3 << 20,
        (HBM, HBM, VM),
    )
    out = call(
        out_kernel,
        (sds((CHUNKS * FROWS, NX), F32), sds((9, 3, CI, CO), F32), sds((1, CO), F32)),
        [],
        [VM],
        1 << 22,
        3 << 20,
    )
    x0, x1 = turn(far(volumes[0]))
    x_low, x_high = neighbours(x0, x1)
    wf, wb, fin = prep(kernel.transpose(0, 1, 2, 4, 3), finished_grads.reshape(2048, NX))
    fin = exchange(fin, PLANE)
    act, g0, g1 = forward(x_low, far(x0), far(x1), x_high, far(wf), bias, far(cotangent[0]))
    g_low, g_high = neighbours(g0, g1)
    taps = weight(x_low, far(x0), far(x1), x_high, far(g0), far(g1))
    taps = exchange(taps.reshape(CHUNKS, TROWS, NX), PLANE)
    joined = join_b(fin, taps)
    joined = exchange(joined, COLUMN)
    joined = join_c(joined)
    joined = exchange(joined, PLANE)
    grad_volumes = back(g_low, far(g0), far(g1), g_high, far(wb))
    summed, grad_taps, grad_bias = out(joined)
    grad_kernel = grad_taps.reshape(3, 3, 3, CI, CO).transpose(0, 1, 2, 4, 3)
    return act[None], grad_volumes[None], grad_kernel, grad_bias.reshape(CO), summed.reshape(-1)


def solution(mesh):
    fine = Mesh(mesh.devices.reshape(2, 4, 8, 2, 2), ("yl", "x", "z", "yh", "c"))
    dp = ("yl", "x")
    slab = P(dp, None, SPACE, None, None)
    return jax.shard_map(
        layer,
        mesh=fine,
        in_specs=(slab, P(), P(), slab, P(dp, SPACE, None)),
        out_specs=(slab, slab, P(), P(), P()),
        check_vma=False,
    )
```

profile of v0, /device:TPU:1, one launch (start us, length us, event | category | flops | bytes accessed | tf_op | source)
XLA Modules:
  0.0 110.5 jit_solution(4957962356040172463)
XLA Ops:
  0.6 0.0 copy-start.2
  0.6 3.5 %shard_map.92 = (bf16[1600,128]{1,0:T(8,128)(2,1)}, bf16[1600,128]{1,0:T(8,128)(2,1)}) custom-call(bf16[32,2,48,128]{3,2,1,0:T(8,128)(2,1)} %bitcast.15), custom_call_target="tpu_custom_call" | custom-call | flops 4194304 | bytes 3145728 | tf_op jit(solution)/shard_map/pallas_call | solution.py:385
  4.1 6.2 %collective-permute-start = (bf16[1600,128]{1,0:T(8,128)(2,1)}, bf16[1600,128]{1,0:T(8,128)(2,1)S(1)}, u32[]{:S(2)}, u32[]{:S(2)}) collective-permute-start(bf16[1600,128]{1,0:T(8,128)(2,1)} %get-tuple-element.16.refs_2_), channel_id=1, source_target_pairs={{0,1},{1,2},{2,3},{3,4},{4,5},{5,6},{6,7},{7,8},{8,9},{9,10},{10,1... | collective-permute-start | bytes 1228808 | tf_op jit(solution)/shard_map/ppermute | solution.py:303
  10.4 1.9 %collective-permute-start.1 = (bf16[1600,128]{1,0:T(8,128)(2,1)}, bf16[1600,128]{1,0:T(8,128)(2,1)S(1)}, u32[]{:S(2)}, u32[]{:S(2)}) collective-permute-start(bf16[1600,128]{1,0:T(8,128)(2,1)} %get-tuple-element.17.refs_1_), channel_id=1, source_target_pairs={{1,0},{2,1},{3,2},{4,3},{5,4},{6,5},{7,6},{8,7},{9,8},{10,9},{11,1... | collective-permute-start | bytes 1228808 | tf_op jit(solution)/shard_map/ppermute | solution.py:303
  12.3 0.0 copy-start
  12.3 1.2 %copy-done = f32[1,1,262144]{2,1,0:T(1,128)S(1)} copy-done((f32[1,1,262144]{2,1,0:T(1,128)S(1)}, f32[1,1,262144]{2,1,0:T(1,128)}, u32[]{:S(2)}) %copy-start) | copy-done | bytes 1048600
  13.5 0.0 copy-start.1
  13.5 0.9 copy-done.1
  14.4 2.0 %shard_map.93 = (bf16[768,512]{1,0:T(8,128)(2,1)}, bf16[192,768]{1,0:T(8,128)(2,1)}, bf16[32,64,128]{2,1,0:T(8,128)(2,1)}) custom-call(bf16[3,3,3,32,64]{4,3,2,1,0:T(8,128)(2,1)S(1)} %bitcast.13, f32[2048,128]{1,0:T(8,128)S(1)} %bitcast.12), custom_call_target="tpu_custom_call" | custom-call | flops 4194304 | bytes 3145728 | tf_op jit(solution)/shard_map/pallas_call | solution.py:387
  16.5 7.5 %all-to-all-start = ((bf16[32,64,128]{2,1,0:T(8,128)(2,1)}), bf16[32,64,128]{2,1,0:T(8,128)(2,1)S(1)}, u32[]{:S(2)}, u32[]{:S(2)}) async-start(bf16[32,64,128]{2,1,0:T(8,128)(2,1)} %get-tuple-element.23), calls=%async_computation | async-start | bytes 1048576 | tf_op jit(solution)/shard_map/all_to_all | solution.py:287
  24.0 0.0 collective-permute-done.refs_0_
  24.0 0.0 collective-permute-done.1.refs_3_
  24.1 0.0 copy-done.2
  24.1 14.9 %shard_map.94 = (bf16[64,2,48,128]{3,2,1,0:T(8,128)(2,1)}, bf16[3200,128]{1,0:T(8,128)(2,1)}, bf16[3200,128]{1,0:T(8,128)(2,1)}) custom-call(bf16[1600,128]{1,0:T(8,128)(2,1)S(1)} %collective-permute-done.refs_0_, bf16[1600,128]{1,0:T(8,128)(2,1)} %get-tuple-element.17.refs_1_, bf16[1600,128]{1,0:T(8,128)(2,1)} %get-tuple-element.16.refs_2_, ...), custom_call_target="tpu_custom_call" | custom-call | flops 12884901888 | bytes 8388608 | tf_op jit(solution)/shard_map/pallas_call | solution.py:389
  39.0 5.0 %collective-permute-start.2 = (bf16[3200,128]{1,0:T(8,128)(2,1)}, bf16[3200,128]{1,0:T(8,128)(2,1)S(1)}, u32[]{:S(2)}, u32[]{:S(2)}) collective-permute-start(bf16[3200,128]{1,0:T(8,128)(2,1)} %get-tuple-element.20.refs_2_.refs_5_), channel_id=1, source_target_pairs={{0,1},{1,2},{2,3},{3,4},{4,5},{5,6},{6,7},{7,8},{8,9},{9,10},{10,1... | collective-permute-start | bytes 2457608 | tf_op jit(solution)/shard_map/ppermute | solution.py:303
  44.1 1.9 %collective-permute-start.3 = (bf16[3200,128]{1,0:T(8,128)(2,1)}, bf16[3200,128]{1,0:T(8,128)(2,1)S(1)}, u32[]{:S(2)}, u32[]{:S(2)}) collective-permute-start(bf16[3200,128]{1,0:T(8,128)(2,1)} %get-tuple-element.21.refs_1_.refs_4_), channel_id=1, source_target_pairs={{1,0},{2,1},{3,2},{4,3},{5,4},{6,5},{7,6},{8,7},{9,8},{10,9},{11,1... | collective-permute-start | bytes 2457608 | tf_op jit(solution)/shard_map/ppermute | solution.py:303
  46.0 11.1 %shard_map.96 = bf16[512,128]{1,0:T(8,128)(2,1)S(1)} custom-call(bf16[1600,128]{1,0:T(8,128)(2,1)S(1)} %collective-permute-done.refs_0_, bf16[1600,128]{1,0:T(8,128)(2,1)} %get-tuple-element.17.refs_1_, bf16[1600,128]{1,0:T(8,128)(2,1)} %get-tuple-element.16.refs_2_, bf16[1600,128]{1,0:T(8,128)(2,1)S(1)} %collective-permute-done.1.refs_3_, ...), custom_call_target="tpu_custom_call" | custom-call | flops 12884901888 | bytes 5242880 | tf_op jit(solution)/shard_map/pallas_call | solution.py:391
  57.1 0.0 all-to-all-done.f_ref
  57.1 14.8 %all_to_all.20.t_ref = bf16[32,16,128]{2,1,0:T(8,128)(2,1)S(1)} all-to-all(bf16[32,16,128]{2,1,0:T(8,128)(2,1)S(1)} %bitcast.14), channel_id=1, replica_groups=mesh['yl'=2,'x'=4,'z'=8,'yh'=2,'c'=2] {'yl','x','yh','c'}, dimensions={0} | all-to-all | bytes 262144 | tf_op jit(solution)/shard_map/all_to_all | solution.py:287
  71.9 0.1 shard_map.97
  72.0 17.7 %all_to_all.21.in_ref = bf16[8,80,128]{2,1,0:T(8,128)(2,1)S(1)} all-to-all(bf16[8,80,128]{2,1,0:T(8,128)(2,1)S(1)} %shard_map.97), channel_id=1, replica_groups=mesh['yl'=2,'x'=4,'z'=8,'yh'=2,'c'=2] {'z'}, dimensions={0} | all-to-all | bytes 327680 | tf_op jit(solution)/shard_map/all_to_all | solution.py:287
  89.7 0.9 shard_map.98
  90.6 5.7 %all-to-all-start.3 = ((bf16[32,80,128]{2,1,0:T(8,128)(2,1)}), bf16[32,80,128]{2,1,0:T(8,128)(2,1)S(1)}, u32[]{:S(2)}, u32[]{:S(2)}) async-start(bf16[32,80,128]{2,1,0:T(8,128)(2,1)} %shard_map.98), calls=%async_computation.3 | async-start | bytes 1310720 | tf_op jit(solution)/shard_map/all_to_all | solution.py:287
  96.3 0.0 collective-permute-done.2.refs_0_
  96.3 0.0 collective-permute-done.3.refs_3_
  96.3 8.5 %shard_map.95 = bf16[32,2,48,128]{3,2,1,0:T(8,128)(2,1)} custom-call(bf16[3200,128]{1,0:T(8,128)(2,1)S(1)} %collective-permute-done.2.refs_0_, bf16[3200,128]{1,0:T(8,128)(2,1)} %get-tuple-element.21.refs_1_.refs_4_, bf16[3200,128]{1,0:T(8,128)(2,1)} %get-tuple-element.20.refs_2_.refs_5_, bf16[3200,128]{1,0:T(8,128)(2,1)S(1)} %collective-permute-done.3.refs_3_, ...), custom_call_target="tpu_custom_call" | custom-call | flops 12884901888 | bytes 8388608 | tf_op jit(solution)/shard_map/pallas_call | solution.py:397
  104.8 4.5 %all-to-all-done.3.in_ref = bf16[32,80,128]{2,1,0:T(8,128)(2,1)S(1)} async-done(((bf16[32,80,128]{2,1,0:T(8,128)(2,1)}), bf16[32,80,128]{2,1,0:T(8,128)(2,1)S(1)}, u32[]{:S(2)}, u32[]{:S(2)}) %all-to-all-start.3) | async-done | bytes 655392 | tf_op jit(solution)/shard_map/all_to_all | solution.py:287
  109.3 1.2 %shard_map.99 = (f32[2048,128]{1,0:T(8,128)}, f32[9,3,32,64]{3,2,1,0:T(8,128)}, f32[1,64]{1,0:T(1,128)}) custom-call(bf16[32,80,128]{2,1,0:T(8,128)(2,1)S(1)} %all-to-all-done.3.in_ref), custom_call_target="tpu_custom_call" | custom-call | flops 4194304 | bytes 3145728 | tf_op jit(solution)/shard_map/pallas_call | solution.py:398
Async XLA Ops:
  0.6 23.4 %copy-start.2 = (f32[64]{0:T(128)S(1)}, f32[64]{0:T(128)}, u32[]{:S(2)}) copy-start(f32[64]{0:T(128)} %refs_5_.1) | copy-start | bytes 772
  4.1 19.9 %collective-permute-start = (bf16[1600,128]{1,0:T(8,128)(2,1)}, bf16[1600,128]{1,0:T(8,128)(2,1)S(1)}, u32[]{:S(2)}, u32[]{:S(2)}) collective-permute-start(bf16[1600,128]{1,0:T(8,128)(2,1)} %get-tuple-element.16.refs_2_), channel_id=1, source_target_pairs={{0,1},{1,2},{2,3},{3,4},{4,5},{5,6},{6,7},{7,8},{8,9},{9,10},{10,1... | collective-permute-start | bytes 1228808 | tf_op jit(solution)/shard_map/ppermute | solution.py:303
  10.4 13.7 %collective-permute-start.1 = (bf16[1600,128]{1,0:T(8,128)(2,1)}, bf16[1600,128]{1,0:T(8,128)(2,1)S(1)}, u32[]{:S(2)}, u32[]{:S(2)}) collective-permute-start(bf16[1600,128]{1,0:T(8,128)(2,1)} %get-tuple-element.17.refs_1_), channel_id=1, source_target_pairs={{1,0},{2,1},{3,2},{4,3},{5,4},{6,5},{7,6},{8,7},{9,8},{10,9},{11,1... | collective-permute-start | bytes 1228808 | tf_op jit(solution)/shard_map/ppermute | solution.py:303
  12.3 1.2 %copy-start = (f32[1,1,262144]{2,1,0:T(1,128)S(1)}, f32[1,1,262144]{2,1,0:T(1,128)}, u32[]{:S(2)}) copy-start(f32[1,1,262144]{2,1,0:T(1,128)} %param.9) | copy-start | bytes 3145732
  13.5 0.9 copy-start.1
  16.5 40.6 %all-to-all-start = ((bf16[32,64,128]{2,1,0:T(8,128)(2,1)}), bf16[32,64,128]{2,1,0:T(8,128)(2,1)S(1)}, u32[]{:S(2)}, u32[]{:S(2)}) async-start(bf16[32,64,128]{2,1,0:T(8,128)(2,1)} %get-tuple-element.23), calls=%async_computation | async-start | bytes 1048576 | tf_op jit(solution)/shard_map/all_to_all | solution.py:287
  39.0 57.3 %collective-permute-start.2 = (bf16[3200,128]{1,0:T(8,128)(2,1)}, bf16[3200,128]{1,0:T(8,128)(2,1)S(1)}, u32[]{:S(2)}, u32[]{:S(2)}) collective-permute-start(bf16[3200,128]{1,0:T(8,128)(2,1)} %get-tuple-element.20.refs_2_.refs_5_), channel_id=1, source_target_pairs={{0,1},{1,2},{2,3},{3,4},{4,5},{5,6},{6,7},{7,8},{8,9},{9,10},{10,1... | collective-permute-start | bytes 2457608 | tf_op jit(solution)/shard_map/ppermute | solution.py:303
  44.1 52.2 %collective-permute-start.3 = (bf16[3200,128]{1,0:T(8,128)(2,1)}, bf16[3200,128]{1,0:T(8,128)(2,1)S(1)}, u32[]{:S(2)}, u32[]{:S(2)}) collective-permute-start(bf16[3200,128]{1,0:T(8,128)(2,1)} %get-tuple-element.21.refs_1_.refs_4_), channel_id=1, source_target_pairs={{1,0},{2,1},{3,2},{4,3},{5,4},{6,5},{7,6},{8,7},{9,8},{10,9},{11,1... | collective-permute-start | bytes 2457608 | tf_op jit(solution)/shard_map/ppermute | solution.py:303
  90.6 18.7 %all-to-all-start.3 = ((bf16[32,80,128]{2,1,0:T(8,128)(2,1)}), bf16[32,80,128]{2,1,0:T(8,128)(2,1)S(1)}, u32[]{:S(2)}, u32[]{:S(2)}) async-start(bf16[32,80,128]{2,1,0:T(8,128)(2,1)} %shard_map.98), calls=%async_computation.3 | async-start | bytes 1310720 | tf_op jit(solution)/shard_map/all_to_all | solution.py:287
where the time goes:
time: 111 us
  Pallas kernels  42.3 us (38%)
  blocking collectives  32.5 us (29%)
  starting transfers between devices  28.3 us (25%)
  waiting for transfers between devices  4.51 us (4%)
  local copies, waits for them, and re-layouts  2.16 us (2%)
    all_to_all x2, blocking collectives, exchange(): return lax.all_to_all(parts, axes, 0, 0)  32.5 us
    ppermute x4, starting transfers between devices, neighbours(): return (lax.ppermute(high, SPACE, up), lax.ppermute(low, SPACE, down))  15.1 us
    pallas_call x1, Pallas kernels, layer(): forward(x_low, far(x0), far(x1), x_high, far(wf), bias, far(cotangent[0]))  14.9 us
    all_to_all x2, starting transfers between devices, exchange(): return lax.all_to_all(parts, axes, 0, 0)  13.2 us
    pallas_call x1, Pallas kernels, layer(): taps = weight(x_low, far(x0), far(x1), x_high, far(g0), far(g1))  11.1 us
    pallas_call x1, Pallas kernels, layer(): grad_volumes = back(g_low, far(g0), far(g1), g_high, far(wb))  8.46 us
    all_to_all x2, waiting for transfers between devices, exchange(): return lax.all_to_all(parts, axes, 0, 0)  4.5 us
    pallas_call x1, Pallas kernels, layer(): x0, x1 = turn(far(volumes[0]))  3.5 us
  transfers between devices with their start and end apart: 6, of which 1 were waited for; matrix products, arithmetic and copies ran while one was open for 0% of the time, Pallas kernels for 34%

commit v1 on v0

--- a/solution.py
+++ b/solution.py
@@ -36,26 +36,42 @@
 DMA = pltpu.SemaphoreType.DMA
 
 
-def turn_kernel(x_ref, p0_ref, p1_ref, x, s0, s1, b0, b1, in_sem, out_sem):
+def by_core(copy_pairs, sems):
+    core = lax.axis_index("c")
+    for n, pairs in enumerate(copy_pairs):
+        for side, (src, dst) in enumerate(pairs):
+
+            @pl.when(core == side)
+            def _(src=src, dst=dst, n=n):
+                pltpu.make_async_copy(src, dst, sems.at[n]).start()
+
+    return [pltpu.make_async_copy(*pairs[0], sems.at[n]) for n, pairs in enumerate(copy_pairs)]
+
+
+def turn_kernel(x_ref, inner_ref, outer_ref, x, s0, s1, b0, b1, in_sem, out_sem):
     parts = [
-        pltpu.make_async_copy(x_ref.at[pl.ds(8 * n, 8)], x.at[pl.ds(8 * n, 8)], in_sem.at[n])
-        for n in range(4)
+        [
+            pltpu.make_async_copy(
+                x_ref.at[pl.ds(16 * n, 16), z], x.at[pl.ds(16 * n, 16), z], in_sem.at[2 * z + n]
+            )
+            for n in range(2)
+        ]
+        for z in range(2)
     ]
-    for part in parts:
+    for part in parts[0] + parts[1]:
         part.start()
     for b in (b0, b1):
         b[0:CI, :] = jnp.zeros((CI, NX), BF)
         b[CI * (NY + 1) : CI * PADY, :] = jnp.zeros((CI, NX), BF)
-    for n, part in enumerate(parts):
-        part.wait()
-        for c in range(8 * n, 8 * n + 8):
-            for z, s in ((0, s0), (1, s1)):
+    outs = []
+    for z, (s, b) in enumerate(((s0, b0), (s1, b1))):
+        for n in range(2):
+            parts[z][n].wait()
+            for c in range(16 * n, 16 * n + 16):
                 s[pl.ds(c, NY, stride=CI), :] = x[c, z].astype(F32)
-    outs = []
-    for n, (p, s, b) in enumerate(((p0_ref, s0, b0), (p1_ref, s1, b1))):
         b[CI : CI * (NY + 1), :] = s[...].astype(BF)
-        outs.append(pltpu.make_async_copy(b, p, out_sem.at[n]))
-        outs[-1].start()
+        first, second = (outer_ref, inner_ref) if z == 0 else (inner_ref, outer_ref)
+        outs += by_core([((b, first), (b, second))], out_sem.at[pl.ds(z, 1)])
     for out in outs:
         out.wait()
 
@@ -70,14 +86,18 @@
 HALF = NY // 2 + 2
 
 
-def halves(planes, buffers, width, sems):
-    first, second = [], []
-    for n, (p, b) in enumerate(zip(planes, buffers)):
-        for part, rows, at in ((first, pl.ds(0, HALF * width), 0), (second, pl.ds(HALF * width, (PADY - HALF) * width), 1)):
-            part.append(pltpu.make_async_copy(p.at[rows], b.at[rows], sems.at[2 * n + at]))
-    for copy in first + second:
-        copy.start()
-    return first, second
+def halves(sources, buffers, width, sems):
+    waits = []
+    for half, rows in enumerate((pl.ds(0, HALF * width), pl.ds(HALF * width, (PADY - HALF) * width))):
+        pairs = [
+            tuple((src.at[rows], b.at[rows]) for src in both) for both, b in zip(sources, buffers)
+        ]
+        waits.append(by_core(pairs, sems.at[pl.ds(half * len(buffers), len(buffers))]))
+    return waits
+
+
+def x_sources(far_inner, far_outer, inner, outer):
+    return ((far_outer, far_inner), (outer, inner), (inner, outer), (far_inner, far_outer))
 
 
 def forward_kernel(*refs):
@@ -85,7 +105,7 @@
     planes, (a, cot, act, g0, g1, s0, s1, in_sem, act_sem) = refs[10:14], refs[14:]
     a_copy = pltpu.make_async_copy(a_ref, a, in_sem.at[8])
     a_copy.start()
-    first, second = halves(p_refs, planes, CI, in_sem)
+    first, second = halves(x_sources(*p_refs), planes, CI, in_sem)
     cot_copy = pltpu.make_async_copy(cot_ref, cot, in_sem.at[9])
     cot_copy.start()
     for g in (g0, g1):
@@ -142,8 +162,8 @@
 def weight_kernel(*refs):
     p_refs, g_refs, out_ref = refs[:4], refs[4:6], refs[6]
     planes, gs_buf, acc, sems = refs[7:11], refs[11:13], refs[13], refs[14]
-    first, second = halves(p_refs, planes, CI, sems)
-    g_first, g_second = halves(g_refs, gs_buf, CO, sems.at[pl.ds(8, 4)])
+    first, second = halves(x_sources(*p_refs), planes, CI, sems)
+    g_first, g_second = halves([(g, g) for g in g_refs], gs_buf, CO, sems.at[pl.ds(8, 4)])
     acc[...] = jnp.zeros_like(acc)
     lane = lax.broadcasted_iota(jnp.int32, (CO, NX), 1)
 
@@ -184,28 +204,26 @@
     out_ref[464:512, :] = jnp.zeros((48, NX), BF)
 
 
-def back_kernel(*refs):
-    p_refs, d_ref, out_ref = refs[:4], refs[4], refs[5]
-    planes, (d, buf, s0, s1, sems, out_sem) = refs[6:10], refs[10:]
-    d_copy = pltpu.make_async_copy(d_ref, d, sems.at[8])
+def back_kernel(g0_ref, g1_ref, d_ref, own0_ref, own1_ref, inner_ref, outer_ref, *rest):
+    g0, g1, d, s0, s1, low, high, sems, out_sem = rest
+    d_copy = pltpu.make_async_copy(d_ref, d, sems.at[4])
     d_copy.start()
-    first, second = halves(p_refs, planes, CO, sems)
+    first, second = halves([(g0_ref, g0_ref), (g1_ref, g1_ref)], (g0, g1), CO, sems)
 
     def conv(q, _):
-        for z, s in ((0, s0), (1, s1)):
-            sides = []
+        r = []
+        for g in (g0, g1):
+            sides = [
+                g[pl.ds(pl.multiple_of((2 * q + h) * (2 * CO), 2 * CO), 4 * CO), :] for h in range(2)
+            ]
+            r.append(jnp.dot(d[...], jnp.concatenate(sides, axis=1), preferred_element_type=F32))
+        volumes = (r[0][0:192], r[0][192:384] + r[1][0:192], r[0][384:576] + r[1][192:384], r[1][384:576])
+        for v, s in zip(volumes, (low, s0, s1, high)):
             for h in range(2):
-                start = pl.multiple_of((2 * q + h) * (2 * CO), 2 * CO)
-                sides.append(
-                    jnp.concatenate(
-                        [planes[z + 2 - i][pl.ds(start, 4 * CO), :] for i in range(3)], axis=0
-                    )
-                )
-            r = jnp.dot(d[...], jnp.concatenate(sides, axis=1), preferred_element_type=F32)
-            for h in range(2):
-                rr = r[:, NX * h : NX * (h + 1)]
+                rr = v[:, NX * h : NX * (h + 1)]
                 at = pl.multiple_of((2 * q + h) * (2 * CI), 2 * CI)
-                s[pl.ds(at, 2 * CI), :] = shifted_sum(rr[128:192], rr[64:128], rr[0:64])
+                y = shifted_sum(rr[128:192], rr[64:128], rr[0:64])
+                s[pl.ds(at, 2 * CI), :] = y.astype(s.dtype)
         return 0
 
     d_copy.wait()
@@ -213,6 +231,28 @@
         for copy in part:
             copy.wait()
         lax.fori_loop(lo, lo + 6, conv, 0)
+    outs = by_core(
+        [((high, inner_ref), (low, inner_ref)), ((low, outer_ref), (high, outer_ref))],
+        out_sem.at[pl.ds(0, 2)],
+    )
+    for n, (s, own) in enumerate(((s0, own0_ref), (s1, own1_ref))):
+        outs.append(pltpu.make_async_copy(s, own, out_sem.at[2 + n]))
+        outs[-1].start()
+    for out in outs:
+        out.wait()
+
+
+def finish_kernel(own0_ref, own1_ref, inner_ref, outer_ref, out_ref, s0, s1, e0, e1, buf, sems, out_sem):
+    loads = by_core(
+        [((outer_ref, e0), (inner_ref, e0)), ((inner_ref, e1), (outer_ref, e1))], sems.at[pl.ds(0, 2)]
+    )
+    for n, (own, s) in enumerate(((own0_ref, s0), (own1_ref, s1))):
+        loads.append(pltpu.make_async_copy(own, s, sems.at[2 + n]))
+        loads[-1].start()
+    for load in loads:
+        load.wait()
+    for s, e in ((s0, e0), (s1, e1)):
+        s[...] += e[...].astype(F32)
 
     def gather(c, _):
         for z, s in ((0, s0), (1, s1)):
@@ -229,8 +269,16 @@
         out.wait()
 
 
-def prep_kernel(w_ref, f_ref, a_out, d_out, out_ref, turned, a_ref, d_ref, sem):
-    out_ref[...] = f_ref[...].reshape(CHUNKS, FROWS, NX).astype(BF)
+def prep_kernel(w_hbm, f_hbm, a_out, d_out, out_ref, turned, a_ref, d_ref, w_ref, f_ref, sem):
+    w_copy = pltpu.make_async_copy(w_hbm, w_ref, sem.at[2])
+    w_copy.start()
+    f_copies = [
+        pltpu.make_async_copy(f_hbm.at[pl.ds(512 * n, 512)], f_ref.at[pl.ds(512 * n, 512)], sem.at[3 + n])
+        for n in range(4)
+    ]
+    for copy in f_copies:
+        copy.start()
+    w_copy.wait()
     for z, hole in ((0, 3), (1, 0)):
         for k in range(3):
             col = (k * 2 + z) * 128
@@ -242,7 +290,7 @@
             for s in range(4):
                 pair = jnp.concatenate([w[s] if s < 3 else none, w[s - 1] if s else none], axis=1)
                 y, p = ((0, 1), (1, 1), (0, 0), (1, 0))[s]
-                row, col = (k * 2 + y) * CI, i * 256 + p * 128
+                row, col = i * 192 + (k * 2 + y) * CI, p * 128
                 d_ref[row : row + CI, col : col + 128] = pair.astype(BF)
                 for z in range(2):
                     row, col = ((i + z) * 4 + s) * CI, (k * 2 + z) * 128
@@ -252,6 +300,10 @@
     a_ref[...] = turned[...].T.astype(BF)
     a_copy = pltpu.make_async_copy(a_ref, a_out, sem.at[1])
     a_copy.start()
+    for n, copy in enumerate(f_copies):
+        copy.wait()
+        part = f_ref[512 * n : 512 * n + 512, :]
+        out_ref[8 * n : 8 * n + 8] = part.reshape(8, FROWS, NX).astype(BF)
     d_copy.wait()
     a_copy.wait()
 
@@ -297,10 +349,10 @@
     return call(join_c_kernel, sds, [], [VM], 1 << 20, 1 << 20)(parts)
 
 
-def neighbours(low, high):
-    up = [(i, i + 1) for i in range(31)]
-    down = [(i + 1, i) for i in range(31)]
-    return lax.ppermute(high, SPACE, up), lax.ppermute(low, SPACE, down)
+def swap(inner, outer):
+    on_chip = [(i, i ^ 1) for i in range(32)]
+    off_chip = [(i, i + 1) for i in range(1, 31, 2)] + [(i + 1, i) for i in range(1, 31, 2)]
+    return lax.ppermute(inner, SPACE, on_chip), lax.ppermute(outer, SPACE, off_chip)
 
 
 def far(x):
@@ -335,7 +387,7 @@
         + [gbuf] * 2
         + [pltpu.VMEM((NY * CO, NX), F32)] * 2
         + [DMA((10,)), DMA((6,))],
-        [ANY, HBM, HBM, ANY, HBM, pl.BlockSpec(memory_space=pltpu.SMEM), HBM],
+        [ANY, ANY, HBM, HBM, HBM, pl.BlockSpec(memory_space=pltpu.SMEM), HBM],
         3 << 32,
         8 << 20,
         (HBM, HBM, HBM),
@@ -344,32 +396,47 @@
         weight_kernel,
         sds((512, NX), BF),
         [xbuf] * 4 + [gbuf] * 2 + [pltpu.VMEM((304, 192), F32), DMA((12,))],
-        [ANY, HBM, HBM, ANY, HBM, HBM],
+        [ANY, ANY, HBM, HBM, HBM, HBM],
         3 << 32,
         5 << 20,
     )
+    edge = (NY * CI, NX)
     back = call(
         back_kernel,
-        pltpu.HBM((CI, 2, NY, NX), BF),
-        [gbuf] * 4
-        + [pltpu.VMEM((192, 768), BF), pltpu.VMEM((CI, 2, NY, NX), BF)]
-        + [pltpu.VMEM((NY * CI, NX), F32)] * 2
-        + [DMA((9,)), DMA((2,))],
-        [ANY, HBM, HBM, ANY, HBM],
+        (pltpu.HBM(edge, F32), pltpu.HBM(edge, F32), pltpu.HBM(edge, BF), pltpu.HBM(edge, BF)),
+        [gbuf] * 2
+        + [pltpu.VMEM((576, 256), BF)]
+        + [pltpu.VMEM(edge, F32)] * 2
+        + [pltpu.VMEM(edge, BF)] * 2
+        + [DMA((5,)), DMA((4,))],
+        [HBM] * 3,
         3 << 32,
         8 << 20,
+        (HBM,) * 4,
+    )
+    finish = call(
+        finish_kernel,
+        pltpu.HBM((CI, 2, NY, NX), BF),
+        [pltpu.VMEM(edge, F32)] * 2
+        + [pltpu.VMEM(edge, BF)] * 2
+        + [pltpu.VMEM((CI, 2, NY, NX), BF), DMA((4,)), DMA((2,))],
+        [HBM, HBM, ANY, ANY],
+        1 << 28,
+        4 << 20,
         HBM,
     )
     prep = call(
         prep_kernel,
-        (pltpu.HBM((768, 512), BF), pltpu.HBM((192, 768), BF), sds((CHUNKS, FROWS, NX), BF)),
+        (pltpu.HBM((768, 512), BF), pltpu.HBM((576, 256), BF), sds((CHUNKS, FROWS, NX), BF)),
         [
             pltpu.VMEM((512, 768), F32),
             pltpu.VMEM((768, 512), BF),
-            pltpu.VMEM((192, 768), BF),
-            DMA((2,)),
+            pltpu.VMEM((576, 256), BF),
+            pltpu.VMEM((3, 3, 3, CI, CO), BF),
+            pltpu.VMEM((2048, NX), F32),
+            DMA((7,)),
         ],
-        [VM] * 2,
+        [HBM] * 2,
         1 << 22,
         3 << 20,
         (HBM, HBM, VM),
@@ -382,19 +449,21 @@
         1 << 22,
         3 << 20,
     )
-    x0, x1 = turn(far(volumes[0]))
-    x_low, x_high = neighbours(x0, x1)
-    wf, wb, fin = prep(kernel.transpose(0, 1, 2, 4, 3), finished_grads.reshape(2048, NX))
+    inner, outer = turn(far(volumes[0]))
+    far_inner, far_outer = swap(inner, outer)
+    wf, wb, fin = prep(far(kernel.transpose(0, 1, 2, 4, 3)), far(finished_grads.reshape(2048, NX)))
     fin = exchange(fin, PLANE)
-    act, g0, g1 = forward(x_low, far(x0), far(x1), x_high, far(wf), bias, far(cotangent[0]))
-    g_low, g_high = neighbours(g0, g1)
-    taps = weight(x_low, far(x0), far(x1), x_high, far(g0), far(g1))
+    x = (far_inner, far_outer, far(inner), far(outer))
+    act, g0, g1 = forward(*x, far(wf), bias, far(cotangent[0]))
+    taps = weight(*x, far(g0), far(g1))
     taps = exchange(taps.reshape(CHUNKS, TROWS, NX), PLANE)
+    own0, own1, inner, outer = back(far(g0), far(g1), far(wb))
+    far_inner, far_outer = swap(inner, outer)
     joined = join_b(fin, taps)
     joined = exchange(joined, COLUMN)
     joined = join_c(joined)
     joined = exchange(joined, PLANE)
-    grad_volumes = back(g_low, far(g0), far(g1), g_high, far(wb))
+    grad_volumes = finish(far(own0), far(own1), far_inner, far_outer)
     summed, grad_taps, grad_bias = out(joined)
     grad_kernel = grad_taps.reshape(3, 3, 3, CI, CO).transpose(0, 1, 2, 4, 3)
     return act[None], grad_volumes[None], grad_kernel, grad_bias.reshape(CO), summed.reshape(-1)

time: 111 us -> 115 us (1.036)
  waiting for transfers between devices: 4.51 us -> 9.35 us
  starting transfers between devices: 28.3 us -> 23.7 us
  Pallas kernels: 42.3 us -> 46.1 us
  local copies, waits for them, and re-layouts: 2.16 us -> 0.01 us
  blocking collectives: 32.5 us -> 34.3 us
    ppermute x4, waiting for transfers between devices: 0.01 us -> 9.34 us  [the longest x2 9.34 us: swap(): lax.ppermute(outer, SPACE, off_chip)]
    all_to_all x2, waiting for transfers between devices: 4.5 us -> 0.01 us  [exchange(): return lax.all_to_all(parts, axes, 0, 0)]
    pallas_call x5 -> x6, Pallas kernels: 40 us -> 43.9 us  [the longest x1 15 us: layer(): act, g0, g1 = forward(*x, far(wf), bias, far(cotangent[0]))]
    ppermute x4, starting transfers between devices: 15.1 us -> 11.6 us  [the longest x2 7.82 us: swap(): lax.ppermute(outer, SPACE, off_chip)]
    unnamed x6 -> x2, local copies, waits for them, and re-layouts: 2.16 us -> 0.01 us
    all_to_all x2, blocking collectives: 32.5 us -> 34.3 us  [exchange(): return lax.all_to_all(parts, axes, 0, 0)]
  transfers between devices with their start and end apart: 6 -> 6, of which waited for: 1 -> 2; matrix products, arithmetic and copies ran while one was open for 0% -> 0% of each run, Pallas kernels for 34% -> 35%
where the time goes in v1:
time: 115 us; the launch traced here: 114 us
  Pallas kernels  46.1 us (40%)
  blocking collectives  34.3 us (30%)
  starting transfers between devices  23.7 us (21%)
  waiting for transfers between devices  9.35 us (8%)
    all_to_all x2, blocking collectives, exchange(): return lax.all_to_all(parts, axes, 0, 0)  34.3 us
    pallas_call x1, Pallas kernels, layer(): act, g0, g1 = forward(*x, far(wf), bias, far(cotangent[0]))  15 us
    all_to_all x2, starting transfers between devices, exchange(): return lax.all_to_all(parts, axes, 0, 0)  12.1 us
    pallas_call x1, Pallas kernels, layer(): taps = weight(*x, far(g0), far(g1))  11.1 us
    ppermute x2, waiting for transfers between devices, swap(): lax.ppermute(outer, SPACE, off_chip)  9.34 us
    ppermute x2, starting transfers between devices, swap(): lax.ppermute(outer, SPACE, off_chip)  7.82 us
    pallas_call x1, Pallas kernels, layer(): own0, own1, inner, outer = back(far(g0), far(g1), far(wb))  7.56 us
    pallas_call x1, Pallas kernels, layer(): grad_volumes = finish(far(own0), far(own1), far_inner, far_outer)  3.89 us
  transfers between devices with their start and end apart: 6, of which 2 were waited for; matrix products, arithmetic and copies ran while one was open for 0% of the time, Pallas kernels for 35%

profile of v1, /device:TPU:1, one launch (start us, length us, event | category | flops | bytes accessed | tf_op | source)
XLA Modules:
  0.0 114.2 jit_solution(6786256558477602001)
XLA Ops:
  0.6 0.0 copy-start
  0.6 3.3 %shard_map.92 = (bf16[1600,128]{1,0:T(8,128)(2,1)}, bf16[1600,128]{1,0:T(8,128)(2,1)}) custom-call(bf16[32,2,48,128]{3,2,1,0:T(8,128)(2,1)} %bitcast.14), custom_call_target="tpu_custom_call" | custom-call | flops 4194304 | bytes 3145728 | tf_op jit(solution)/shard_map/pallas_call | solution.py:452
  4.0 3.3 %collective-permute-start = (bf16[1600,128]{1,0:T(8,128)(2,1)}, bf16[1600,128]{1,0:T(8,128)(2,1)S(1)}, u32[]{:S(2)}, u32[]{:S(2)}) collective-permute-start(bf16[1600,128]{1,0:T(8,128)(2,1)} %get-tuple-element.20.refs_2_), channel_id=1, source_target_pairs={{0,1},{1,0},{2,3},{3,2},{4,5},{5,4},{6,7},{7,6},{8,9},{9,8},{10,11... | collective-permute-start | bytes 1228808 | tf_op jit(solution)/shard_map/ppermute | solution.py:355
  7.3 3.0 %collective-permute-start.1 = (bf16[1600,128]{1,0:T(8,128)(2,1)}, bf16[1600,128]{1,0:T(8,128)(2,1)S(1)}, u32[]{:S(2)}, u32[]{:S(2)}) collective-permute-start(bf16[1600,128]{1,0:T(8,128)(2,1)} %get-tuple-element.21.refs_3_), channel_id=1, source_target_pairs={{1,2},{3,4},{5,6},{7,8},{9,10},{11,12},{13,14},{15,16},{17,18},{19... | collective-permute-start | bytes 1228808 | tf_op jit(solution)/shard_map/ppermute | solution.py:355
  10.3 3.0 %shard_map.93 = (bf16[768,512]{1,0:T(8,128)(2,1)}, bf16[576,256]{1,0:T(8,128)(2,1)}, bf16[32,64,128]{2,1,0:T(8,128)(2,1)}) custom-call(bf16[3,3,3,32,64]{4,3,2,1,0:T(8,128)(2,1)} %bitcast.16, f32[2048,128]{1,0:T(8,128)} %bitcast.13), custom_call_target="tpu_custom_call" | custom-call | flops 4194304 | bytes 3145728 | tf_op jit(solution)/shard_map/pallas_call | solution.py:454
  13.3 6.4 %all-to-all-start = ((bf16[32,64,128]{2,1,0:T(8,128)(2,1)}), bf16[32,64,128]{2,1,0:T(8,128)(2,1)S(1)}, u32[]{:S(2)}, u32[]{:S(2)}) async-start(bf16[32,64,128]{2,1,0:T(8,128)(2,1)} %get-tuple-element.31), calls=%async_computation | async-start | bytes 1048576 | tf_op jit(solution)/shard_map/all_to_all | solution.py:339
  19.7 0.0 collective-permute-done.refs_0_
  19.7 0.1 collective-permute-done.1.refs_1_
  19.9 0.0 copy-done
  19.9 15.0 %shard_map.94 = (bf16[64,2,48,128]{3,2,1,0:T(8,128)(2,1)}, bf16[3200,128]{1,0:T(8,128)(2,1)}, bf16[3200,128]{1,0:T(8,128)(2,1)}) custom-call(bf16[1600,128]{1,0:T(8,128)(2,1)S(1)} %collective-permute-done.refs_0_, bf16[1600,128]{1,0:T(8,128)(2,1)S(1)} %collective-permute-done.1.refs_1_, bf16[1600,128]{1,0:T(8,128)(2,1)} %get-tuple-element.20.refs_2_, ...), custom_call_target="tpu_custom_call" | custom-call | flops 12884901888 | bytes 8388608 | tf_op jit(solution)/shard_map/pallas_call | solution.py:457
  34.8 11.1 %shard_map.97 = bf16[512,128]{1,0:T(8,128)(2,1)S(1)} custom-call(bf16[1600,128]{1,0:T(8,128)(2,1)S(1)} %collective-permute-done.refs_0_, bf16[1600,128]{1,0:T(8,128)(2,1)S(1)} %collective-permute-done.1.refs_1_, bf16[1600,128]{1,0:T(8,128)(2,1)} %get-tuple-element.20.refs_2_, bf16[1600,128]{1,0:T(8,128)(2,1)} %get-tuple-element.21.refs_3_, ...), custom_call_target="tpu_custom_call" | custom-call | flops 12884901888 | bytes 5242880 | tf_op jit(solution)/shard_map/pallas_call | solution.py:458
  46.0 0.0 all-to-all-done.f_ref
  46.0 15.5 %all_to_all.20.t_ref = bf16[32,16,128]{2,1,0:T(8,128)(2,1)S(1)} all-to-all(bf16[32,16,128]{2,1,0:T(8,128)(2,1)S(1)} %bitcast.12), channel_id=1, replica_groups=mesh['yl'=2,'x'=4,'z'=8,'yh'=2,'c'=2] {'yl','x','yh','c'}, dimensions={0} | all-to-all | bytes 262144 | tf_op jit(solution)/shard_map/all_to_all | solution.py:339
  61.5 0.1 shard_map.98
  61.6 18.8 %all_to_all.21.in_ref = bf16[8,80,128]{2,1,0:T(8,128)(2,1)S(1)} all-to-all(bf16[8,80,128]{2,1,0:T(8,128)(2,1)S(1)} %shard_map.98), channel_id=1, replica_groups=mesh['yl'=2,'x'=4,'z'=8,'yh'=2,'c'=2] {'z'}, dimensions={0} | all-to-all | bytes 327680 | tf_op jit(solution)/shard_map/all_to_all | solution.py:339
  80.4 0.9 shard_map.99
  81.3 5.7 %all-to-all-start.3 = ((bf16[32,80,128]{2,1,0:T(8,128)(2,1)}), bf16[32,80,128]{2,1,0:T(8,128)(2,1)S(1)}, u32[]{:S(2)}, u32[]{:S(2)}) async-start(bf16[32,80,128]{2,1,0:T(8,128)(2,1)} %shard_map.99), calls=%async_computation.3 | async-start | bytes 1310720 | tf_op jit(solution)/shard_map/all_to_all | solution.py:339
  87.0 7.6 %shard_map.95 = (f32[1536,128]{1,0:T(8,128)}, f32[1536,128]{1,0:T(8,128)}, bf16[1536,128]{1,0:T(8,128)(2,1)}, bf16[1536,128]{1,0:T(8,128)(2,1)}) custom-call(bf16[3200,128]{1,0:T(8,128)(2,1)} %get-tuple-element.24.g0_ref.refs_4_, bf16[3200,128]{1,0:T(8,128)(2,1)} %get-tuple-element.25.g1_ref.refs_5_, bf16[576,256]{1,0:T(8,128)(2,1)} %get-tuple-element.26.d_ref), custom_call_target="tpu_custom_call" | custom-call | flops 12884901888 | bytes 8388608 | tf_op jit(solution)/shard_map/pallas_call | solution.py:460
  94.6 0.4 collective-permute-start.2
  95.0 4.8 %collective-permute-start.3 = (bf16[1536,128]{1,0:T(8,128)(2,1)}, bf16[1536,128]{1,0:T(8,128)(2,1)S(1)}, u32[]{:S(2)}, u32[]{:S(2)}) collective-permute-start(bf16[1536,128]{1,0:T(8,128)(2,1)} %get-tuple-element.30), channel_id=1, source_target_pairs={{1,2},{3,4},{5,6},{7,8},{9,10},{11,12},{13,14},{15,16},{17,18},{19... | collective-permute-start | bytes 1179656 | tf_op jit(solution)/shard_map/ppermute | solution.py:355
  99.8 0.0 collective-permute-done.2.inner_ref
  99.8 9.2 %collective-permute-done.3.outer_ref = bf16[1536,128]{1,0:T(8,128)(2,1)S(1)} collective-permute-done((bf16[1536,128]{1,0:T(8,128)(2,1)}, bf16[1536,128]{1,0:T(8,128)(2,1)S(1)}, u32[]{:S(2)}, u32[]{:S(2)}) %collective-permute-start.3) | collective-permute-done | bytes 393248 | tf_op jit(solution)/shard_map/ppermute | solution.py:355
  109.1 3.9 %shard_map.96 = bf16[32,2,48,128]{3,2,1,0:T(8,128)(2,1)} custom-call(f32[1536,128]{1,0:T(8,128)} %get-tuple-element.27.own0_ref, f32[1536,128]{1,0:T(8,128)} %get-tuple-element.28.own1_ref, bf16[1536,128]{1,0:T(8,128)(2,1)S(1)} %collective-permute-done.2.inner_ref, bf16[1536,128]{1,0:T(8,128)(2,1)S(1)} %collective-permute-done.3.outer_ref), custom_call_target="tpu_custom_call" | custom-call | flops 268435456 | bytes 4194304 | tf_op jit(solution)/shard_map/pallas_call | solution.py:466
  112.9 0.0 all-to-all-done.3.in_ref
  113.0 1.2 %shard_map.100 = (f32[2048,128]{1,0:T(8,128)}, f32[9,3,32,64]{3,2,1,0:T(8,128)}, f32[1,64]{1,0:T(1,128)}) custom-call(bf16[32,80,128]{2,1,0:T(8,128)(2,1)S(1)} %all-to-all-done.3.in_ref), custom_call_target="tpu_custom_call" | custom-call | flops 4194304 | bytes 3145728 | tf_op jit(solution)/shard_map/pallas_call | solution.py:467
Async XLA Ops:
  0.6 19.2 %copy-start = (f32[64]{0:T(128)S(1)}, f32[64]{0:T(128)}, u32[]{:S(2)}) copy-start(f32[64]{0:T(128)} %refs_5_.1) | copy-start | bytes 772
  4.0 15.8 %collective-permute-start = (bf16[1600,128]{1,0:T(8,128)(2,1)}, bf16[1600,128]{1,0:T(8,128)(2,1)S(1)}, u32[]{:S(2)}, u32[]{:S(2)}) collective-permute-start(bf16[1600,128]{1,0:T(8,128)(2,1)} %get-tuple-element.20.refs_2_), channel_id=1, source_target_pairs={{0,1},{1,0},{2,3},{3,2},{4,5},{5,4},{6,7},{7,6},{8,9},{9,8},{10,11... | collective-permute-start | bytes 1228808 | tf_op jit(solution)/shard_map/ppermute | solution.py:355
  7.3 12.6 %collective-permute-start.1 = (bf16[1600,128]{1,0:T(8,128)(2,1)}, bf16[1600,128]{1,0:T(8,128)(2,1)S(1)}, u32[]{:S(2)}, u32[]{:S(2)}) collective-permute-start(bf16[1600,128]{1,0:T(8,128)(2,1)} %get-tuple-element.21.refs_3_), channel_id=1, source_target_pairs={{1,2},{3,4},{5,6},{7,8},{9,10},{11,12},{13,14},{15,16},{17,18},{19... | collective-permute-start | bytes 1228808 | tf_op jit(solution)/shard_map/ppermute | solution.py:355
  13.3 32.7 %all-to-all-start = ((bf16[32,64,128]{2,1,0:T(8,128)(2,1)}), bf16[32,64,128]{2,1,0:T(8,128)(2,1)S(1)}, u32[]{:S(2)}, u32[]{:S(2)}) async-start(bf16[32,64,128]{2,1,0:T(8,128)(2,1)} %get-tuple-element.31), calls=%async_computation | async-start | bytes 1048576 | tf_op jit(solution)/shard_map/all_to_all | solution.py:339
  81.3 31.7 %all-to-all-start.3 = ((bf16[32,80,128]{2,1,0:T(8,128)(2,1)}), bf16[32,80,128]{2,1,0:T(8,128)(2,1)S(1)}, u32[]{:S(2)}, u32[]{:S(2)}) async-start(bf16[32,80,128]{2,1,0:T(8,128)(2,1)} %shard_map.99), calls=%async_computation.3 | async-start | bytes 1310720 | tf_op jit(solution)/shard_map/all_to_all | solution.py:339
  94.6 5.3 %collective-permute-start.2 = (bf16[1536,128]{1,0:T(8,128)(2,1)}, bf16[1536,128]{1,0:T(8,128)(2,1)S(1)}, u32[]{:S(2)}, u32[]{:S(2)}) collective-permute-start(bf16[1536,128]{1,0:T(8,128)(2,1)} %get-tuple-element.29), channel_id=1, source_target_pairs={{0,1},{1,0},{2,3},{3,2},{4,5},{5,4},{6,7},{7,6},{8,9},{9,8},{10,11... | collective-permute-start | bytes 1179656 | tf_op jit(solution)/shard_map/ppermute | solution.py:355
  95.0 14.0 %collective-permute-start.3 = (bf16[1536,128]{1,0:T(8,128)(2,1)}, bf16[1536,128]{1,0:T(8,128)(2,1)S(1)}, u32[]{:S(2)}, u32[]{:S(2)}) collective-permute-start(bf16[1536,128]{1,0:T(8,128)(2,1)} %get-tuple-element.30), channel_id=1, source_target_pairs={{1,2},{3,4},{5,6},{7,8},{9,10},{11,12},{13,14},{15,16},{17,18},{19... | collective-permute-start | bytes 1179656 | tf_op jit(solution)/shard_map/ppermute | solution.py:355

commit v2 on v1

--- a/solution.py
+++ b/solution.py
@@ -34,6 +34,10 @@
 HBM = pl.BlockSpec(memory_space=pltpu.HBM)
 ANY = pl.BlockSpec(memory_space=pl.ANY)
 DMA = pltpu.SemaphoreType.DMA
+
+
+def row_of(y, block, blocks):
+    return pl.multiple_of(((y // 8) * blocks + block) * 64 + (y % 8) * 8, 8)
 
 
 def by_core(copy_pairs, sems):
@@ -68,8 +72,12 @@
         for n in range(2):
             parts[z][n].wait()
             for c in range(16 * n, 16 * n + 16):
-                s[pl.ds(c, NY, stride=CI), :] = x[c, z].astype(F32)
-        b[CI : CI * (NY + 1), :] = s[...].astype(BF)
+                v = x[c, z].astype(F32)
+                for m in range(NY // 8):
+                    s[pl.ds((m * 4 + c // 8) * 64 + c % 8, 8, stride=8), :] = v[8 * m : 8 * m + 8]
+        for y in range(NY):
+            v = [s[pl.ds(((y // 8) * 4 + m) * 64 + (y % 8) * 8, 8), :] for m in range(4)]
+            b[CI * (y + 1) : CI * (y + 2), :] = jnp.concatenate(v, axis=0).astype(BF)
         first, second = (outer_ref, inner_ref) if z == 0 else (inner_ref, outer_ref)
         outs += by_core([((b, first), (b, second))], out_sem.at[pl.ds(z, 1)])
     for out in outs:
@@ -122,38 +130,54 @@
         for h in range(2):
             rr = r[:, NX * h : NX * (h + 1)]
             y = shifted_sum(rr[0:256], rr[256:512], rr[512:768])
-            at = pl.multiple_of((2 * q + h) * 128, 128)
-            s0[pl.ds(at, 128), :] = y[0:128]
-            s1[pl.ds(at, 128), :] = y[128:256]
+            for z, s in enumerate((s0, s1)):
+                for p in range(2):
+                    for m in range(8):
+                        at = row_of(4 * q + 2 * h + p, m, 8)
+                        s[pl.ds(at, 8), :] = y[128 * z + 64 * p + 8 * m : 128 * z + 64 * p + 8 * m + 8]
         return 0
 
     a_copy.wait()
     for part, lo in ((first, 0), (second, 6)):
         for copy in part:
             copy.wait()
-        lax.fori_loop(lo, lo + 6, conv, 0)
+        lax.fori_loop(lo, lo + 6, conv, 0, unroll=2)
     cot_copy.wait()
 
-    def point(o, _):
-        b = bias_ref[o]
-        for z, s in ((0, s0), (1, s1)):
-            v = s[pl.ds(o, NY, stride=CO), :] + b
-            sig = 0.5 + 0.5 * jnp.tanh(0.5 * jnp.abs(v))
-            soft = jnp.maximum(v, 0.0) - jnp.log(sig)
-            act[o, z] = (0.3 * v + 0.7 * soft).astype(BF)
-            slope = 0.3 + 0.7 * jnp.where(v >= 0, sig, 1.0 - sig)
-            s[pl.ds(o, NY, stride=CO), :] = cot[o, z].astype(F32) * slope
+    def point(m, _):
+        for n in range(8):
+            o = m * 8 + n
+            b = bias_ref[o]
+            for z, s in ((0, s0), (1, s1)):
+                for y in range(0, NY // 8, 2):
+                    rows = [pl.ds(((y + u) * 8 + m) * 64 + n, 8, stride=8) for u in range(2)]
+                    v = jnp.concatenate([s[r, :] for r in rows], axis=0) + b
+                    t = jnp.tanh(0.5 * v)
+                    soft = 0.7 * jnp.log(0.5 + 0.5 * jnp.abs(t))
+                    act[o, z, 8 * y : 8 * y + 16, :] = (jnp.maximum(v, 0.3 * v) - soft).astype(BF)
+                    grad = cot[o, z, 8 * y : 8 * y + 16, :].astype(F32) * (0.65 + 0.35 * t)
+                    s[rows[0], :] = grad[0:8]
+                    s[rows[1], :] = grad[8:16]
+        some = pl.ds(8 * m, 8)
+        pltpu.make_async_copy(act.at[some], act_ref.at[some], act_sem.at[m]).start()
         return 0
 
+    lax.fori_loop(0, 8, point, 0)
     outs = []
-    for n in range(4):
-        lax.fori_loop(16 * n, 16 * n + 16, point, 0, unroll=2)
-        some = pl.ds(16 * n, 16)
+    for n in range(8):
+        some = pl.ds(8 * n, 8)
         outs.append(pltpu.make_async_copy(act.at[some], act_ref.at[some], act_sem.at[n]))
-        outs[-1].start()
     for n, (g_ref, g, s) in enumerate(((g0_ref, g0, s0), (g1_ref, g1, s1))):
-        g[CO : CO * (NY + 1), :] = s[...].astype(BF)
-        outs.append(pltpu.make_async_copy(g, g_ref, act_sem.at[4 + n]))
+
+        def rows_of(t, _, g=g, s=s):
+            for y in range(8):
+                v = [s[pl.ds((t * 8 + m) * 64 + y * 8, 8), :] for m in range(8)]
+                at = pl.multiple_of((t * 8 + y + 1) * CO, CO)
+                g[pl.ds(at, CO), :] = jnp.concatenate(v, axis=0).astype(BF)
+            return 0
+
+        lax.fori_loop(0, NY // 8, rows_of, 0)
+        outs.append(pltpu.make_async_copy(g, g_ref, act_sem.at[8 + n]))
         outs[-1].start()
     for out in outs:
         out.wait()
@@ -167,23 +191,24 @@
     acc[...] = jnp.zeros_like(acc)
     lane = lax.broadcasted_iota(jnp.int32, (CO, NX), 1)
 
-    def row(y, _):
+    def rows(q, _):
         gs, xs = [], []
-        ystart = pl.multiple_of(y * CI, CI)
-        gstart = pl.multiple_of((y + 1) * CO, CO)
-        for z, g in enumerate(gs_buf):
-            mid = g[pl.ds(gstart, CO), :]
-            wide = mid.astype(F32)
-            before = jnp.where(lane == NX - 1, 0.0, pltpu.roll(wide, NX - 1, 1)).astype(BF)
-            after = jnp.where(lane == 0, 0.0, pltpu.roll(wide, 1, 1)).astype(BF)
-            gs.append(jnp.concatenate([before, mid, after], axis=0))
-            xs.append(
-                jnp.concatenate(
-                    [planes[z + i][pl.ds(ystart, 3 * CI), :] for i in range(3)]
-                    + [jnp.ones((16, NX), BF)],
-                    axis=0,
+        for y in range(4):
+            ystart = pl.multiple_of((4 * q + y) * CI, CI)
+            gstart = pl.multiple_of((4 * q + y + 1) * CO, CO)
+            for z, g in enumerate(gs_buf):
+                mid = g[pl.ds(gstart, CO), :]
+                wide = mid.astype(F32)
+                before = jnp.where(lane == NX - 1, 0.0, pltpu.roll(wide, NX - 1, 1)).astype(BF)
+                after = jnp.where(lane == 0, 0.0, pltpu.roll(wide, 1, 1)).astype(BF)
+                gs.append(jnp.concatenate([before, mid, after], axis=0))
+                xs.append(
+                    jnp.concatenate(
+                        [planes[z + i][pl.ds(ystart, 3 * CI), :] for i in range(3)]
+                        + [jnp.ones((16, NX), BF)],
+                        axis=0,
+                    )
                 )
-            )
         acc[...] += lax.dot_general(
             jnp.concatenate(xs, axis=1),
             jnp.concatenate(gs, axis=1),
@@ -195,7 +220,7 @@
     for part, lo in ((first + g_first, 0), (second + g_second, 24)):
         for copy in part:
             copy.wait()
-        lax.fori_loop(lo, lo + 24, row, 0, unroll=2)
+        lax.fori_loop(lo // 4, lo // 4 + 6, rows, 0)
     out_ref[0:288, :] = acc[0:288, 0:128].astype(BF)
     side = acc[0:288, 128:192]
     tail = jnp.concatenate([side[160:288], jnp.zeros((32, CO), F32)], axis=0)
@@ -221,16 +246,22 @@
         for v, s in zip(volumes, (low, s0, s1, high)):
             for h in range(2):
                 rr = v[:, NX * h : NX * (h + 1)]
-                at = pl.multiple_of((2 * q + h) * (2 * CI), 2 * CI)
                 y = shifted_sum(rr[128:192], rr[64:128], rr[0:64])
-                s[pl.ds(at, 2 * CI), :] = y.astype(s.dtype)
+                if s.dtype == BF:
+                    at = pl.multiple_of((2 * q + h) * (2 * CI), 2 * CI)
+                    s[pl.ds(at, 2 * CI), :] = y.astype(BF)
+                    continue
+                for p in range(2):
+                    for m in range(4):
+                        at = row_of(4 * q + 2 * h + p, m, 4)
+                        s[pl.ds(at, 8), :] = y[32 * p + 8 * m : 32 * p + 8 * m + 8]
         return 0
 
     d_copy.wait()
     for part, lo in ((first, 0), (second, 6)):
         for copy in part:
             copy.wait()
-        lax.fori_loop(lo, lo + 6, conv, 0)
+        lax.fori_loop(lo, lo + 6, conv, 0, unroll=2)
     outs = by_core(
         [((high, inner_ref), (low, inner_ref)), ((low, outer_ref), (high, outer_ref))],
         out_sem.at[pl.ds(0, 2)],
@@ -251,22 +282,31 @@
         loads[-1].start()
     for load in loads:
         load.wait()
-    for s, e in ((s0, e0), (s1, e1)):
-        s[...] += e[...].astype(F32)
-
-    def gather(c, _):
-        for z, s in ((0, s0), (1, s1)):
-            buf[c, z] = s[pl.ds(c, NY, stride=CI), :].astype(BF)
+
+    def add(t, _):
+        for s, e in ((s0, e0), (s1, e1)):
+            for y in range(8):
+                v = e[pl.ds(pl.multiple_of((t * 8 + y) * CI, CI), CI), :].astype(F32)
+                for m in range(4):
+                    at = pl.ds((t * 4 + m) * 64 + y * 8, 8)
+                    s[at, :] += v[8 * m : 8 * m + 8]
         return 0
 
-    outs = []
-    for n in range(2):
-        lax.fori_loop(16 * n, 16 * n + 16, gather, 0, unroll=4)
-        some = pl.ds(16 * n, 16)
-        outs.append(pltpu.make_async_copy(buf.at[some], out_ref.at[some], out_sem.at[n]))
-        outs[-1].start()
-    for out in outs:
-        out.wait()
+    lax.fori_loop(0, NY // 8, add, 0)
+
+    def gather(m, _):
+        for n in range(8):
+            for z, s in ((0, s0), (1, s1)):
+                v = [s[pl.ds((t * 4 + m) * 64 + n, 8, stride=8), :] for t in range(NY // 8)]
+                buf[m * 8 + n, z] = jnp.concatenate(v, axis=0).astype(BF)
+        some = pl.ds(8 * m, 8)
+        pltpu.make_async_copy(buf.at[some], out_ref.at[some], out_sem.at[m]).start()
+        return 0
+
+    lax.fori_loop(0, 4, gather, 0)
+    for n in range(4):
+        some = pl.ds(8 * n, 8)
+        pltpu.make_async_copy(buf.at[some], out_ref.at[some], out_sem.at[n]).wait()
 
 
 def prep_kernel(w_hbm, f_hbm, a_out, d_out, out_ref, turned, a_ref, d_ref, w_ref, f_ref, sem):
@@ -386,7 +426,7 @@
         + [pltpu.VMEM((CO, 2, NY, NX), BF)] * 2
         + [gbuf] * 2
         + [pltpu.VMEM((NY * CO, NX), F32)] * 2
-        + [DMA((10,)), DMA((6,))],
+        + [DMA((10,)), DMA((10,))],
         [ANY, ANY, HBM, HBM, HBM, pl.BlockSpec(memory_space=pltpu.SMEM), HBM],
         3 << 32,
         8 << 20,
@@ -419,7 +459,7 @@
         pltpu.HBM((CI, 2, NY, NX), BF),
         [pltpu.VMEM(edge, F32)] * 2
         + [pltpu.VMEM(edge, BF)] * 2
-        + [pltpu.VMEM((CI, 2, NY, NX), BF), DMA((4,)), DMA((2,))],
+        + [pltpu.VMEM((CI, 2, NY, NX), BF), DMA((4,)), DMA((4,))],
         [HBM, HBM, ANY, ANY],
         1 << 28,
         4 << 20,

time: 115 us -> 103 us (0.90)
  Pallas kernels: 46.1 us -> 34.1 us
    pallas_call x1, Pallas kernels: 15 us -> 9.98 us  [layer(): act, g0, g1 = forward(*x, far(wf), bias, far(cotangent[0]))]
    pallas_call x1, Pallas kernels: 11.1 us -> 7.55 us  [layer(): taps = weight(*x, far(g0), far(g1))]
    pallas_call x1, Pallas kernels: 7.56 us -> 6.28 us  [layer(): own0, own1, inner, outer = back(far(g0), far(g1), far(wb))]
    pallas_call x1, Pallas kernels: 3.32 us -> 2.13 us  [layer(): inner, outer = turn(far(volumes[0]))]
  transfers between devices with their start and end apart: 6 -> 6, of which waited for: 2 -> 2; matrix products, arithmetic and copies ran while one was open for 0% -> 0% of each run, Pallas kernels for 35% -> 29%
where the time goes in v2:
time: 103 us; the launch traced here: 102 us
  blocking collectives  34.3 us (33%)
  Pallas kernels  34.1 us (33%)
  starting transfers between devices  23.7 us (23%)
  waiting for transfers between devices  9.35 us (9%)
    all_to_all x2, blocking collectives, exchange(): return lax.all_to_all(parts, axes, 0, 0)  34.3 us
    all_to_all x2, starting transfers between devices, exchange(): return lax.all_to_all(parts, axes, 0, 0)  12.1 us
    pallas_call x1, Pallas kernels, layer(): act, g0, g1 = forward(*x, far(wf), bias, far(cotangent[0]))  9.98 us
    ppermute x2, waiting for transfers between devices, swap(): lax.ppermute(outer, SPACE, off_chip)  9.34 us
    ppermute x2, starting transfers between devices, swap(): lax.ppermute(outer, SPACE, off_chip)  7.82 us
    pallas_call x1, Pallas kernels, layer(): taps = weight(*x, far(g0), far(g1))  7.55 us
    pallas_call x1, Pallas kernels, layer(): own0, own1, inner, outer = back(far(g0), far(g1), far(wb))  6.28 us
    ppermute x2, starting transfers between devices, swap(): lax.ppermute(inner, SPACE, on_chip)  3.73 us
  transfers between devices with their start and end apart: 6, of which 2 were waited for; matrix products, arithmetic and copies ran while one was open for 0% of the time, Pallas kernels for 29%

profile of v2, /device:TPU:1, one launch (start us, length us, event | category | flops | bytes accessed | tf_op | source)
XLA Modules:
  0.0 102.2 jit_solution(4051307514304983626)
XLA Ops:
  0.6 0.0 copy-start
  0.6 2.1 %shard_map.92 = (bf16[1600,128]{1,0:T(8,128)(2,1)}, bf16[1600,128]{1,0:T(8,128)(2,1)}) custom-call(bf16[32,2,48,128]{3,2,1,0:T(8,128)(2,1)} %bitcast.14), custom_call_target="tpu_custom_call" | custom-call | flops 4194304 | bytes 3145728 | tf_op jit(solution)/shard_map/pallas_call | solution.py:492
  2.8 3.3 %collective-permute-start = (bf16[1600,128]{1,0:T(8,128)(2,1)}, bf16[1600,128]{1,0:T(8,128)(2,1)S(1)}, u32[]{:S(2)}, u32[]{:S(2)}) collective-permute-start(bf16[1600,128]{1,0:T(8,128)(2,1)} %get-tuple-element.20.refs_2_), channel_id=1, source_target_pairs={{0,1},{1,0},{2,3},{3,2},{4,5},{5,4},{6,7},{7,6},{8,9},{9,8},{10,11... | collective-permute-start | bytes 1228808 | tf_op jit(solution)/shard_map/ppermute | solution.py:395
  6.1 3.0 %collective-permute-start.1 = (bf16[1600,128]{1,0:T(8,128)(2,1)}, bf16[1600,128]{1,0:T(8,128)(2,1)S(1)}, u32[]{:S(2)}, u32[]{:S(2)}) collective-permute-start(bf16[1600,128]{1,0:T(8,128)(2,1)} %get-tuple-element.21.refs_3_), channel_id=1, source_target_pairs={{1,2},{3,4},{5,6},{7,8},{9,10},{11,12},{13,14},{15,16},{17,18},{19... | collective-permute-start | bytes 1228808 | tf_op jit(solution)/shard_map/ppermute | solution.py:395
  9.1 3.0 %shard_map.93 = (bf16[768,512]{1,0:T(8,128)(2,1)}, bf16[576,256]{1,0:T(8,128)(2,1)}, bf16[32,64,128]{2,1,0:T(8,128)(2,1)}) custom-call(bf16[3,3,3,32,64]{4,3,2,1,0:T(8,128)(2,1)} %bitcast.16, f32[2048,128]{1,0:T(8,128)} %bitcast.13), custom_call_target="tpu_custom_call" | custom-call | flops 4194304 | bytes 3145728 | tf_op jit(solution)/shard_map/pallas_call | solution.py:494
  12.1 6.4 %all-to-all-start = ((bf16[32,64,128]{2,1,0:T(8,128)(2,1)}), bf16[32,64,128]{2,1,0:T(8,128)(2,1)S(1)}, u32[]{:S(2)}, u32[]{:S(2)}) async-start(bf16[32,64,128]{2,1,0:T(8,128)(2,1)} %get-tuple-element.31), calls=%async_computation | async-start | bytes 1048576 | tf_op jit(solution)/shard_map/all_to_all | solution.py:379
  18.5 0.0 collective-permute-done.refs_0_
  18.6 0.1 collective-permute-done.1.refs_1_
  18.7 0.0 copy-done
  18.7 10.0 %shard_map.94 = (bf16[64,2,48,128]{3,2,1,0:T(8,128)(2,1)}, bf16[3200,128]{1,0:T(8,128)(2,1)}, bf16[3200,128]{1,0:T(8,128)(2,1)}) custom-call(bf16[1600,128]{1,0:T(8,128)(2,1)S(1)} %collective-permute-done.refs_0_, bf16[1600,128]{1,0:T(8,128)(2,1)S(1)} %collective-permute-done.1.refs_1_, bf16[1600,128]{1,0:T(8,128)(2,1)} %get-tuple-element.20.refs_2_, ...), custom_call_target="tpu_custom_call" | custom-call | flops 12884901888 | bytes 8388608 | tf_op jit(solution)/shard_map/pallas_call | solution.py:497
  28.7 7.5 %shard_map.97 = bf16[512,128]{1,0:T(8,128)(2,1)S(1)} custom-call(bf16[1600,128]{1,0:T(8,128)(2,1)S(1)} %collective-permute-done.refs_0_, bf16[1600,128]{1,0:T(8,128)(2,1)S(1)} %collective-permute-done.1.refs_1_, bf16[1600,128]{1,0:T(8,128)(2,1)} %get-tuple-element.20.refs_2_, bf16[1600,128]{1,0:T(8,128)(2,1)} %get-tuple-element.21.refs_3_, ...), custom_call_target="tpu_custom_call" | custom-call | flops 12884901888 | bytes 5242880 | tf_op jit(solution)/shard_map/pallas_call | solution.py:498
  36.2 0.0 all-to-all-done.f_ref
  36.2 15.5 %all_to_all.20.t_ref = bf16[32,16,128]{2,1,0:T(8,128)(2,1)S(1)} all-to-all(bf16[32,16,128]{2,1,0:T(8,128)(2,1)S(1)} %bitcast.12), channel_id=1, replica_groups=mesh['yl'=2,'x'=4,'z'=8,'yh'=2,'c'=2] {'yl','x','yh','c'}, dimensions={0} | all-to-all | bytes 262144 | tf_op jit(solution)/shard_map/all_to_all | solution.py:379
  51.7 0.1 shard_map.98
  51.8 18.9 %all_to_all.21.in_ref = bf16[8,80,128]{2,1,0:T(8,128)(2,1)S(1)} all-to-all(bf16[8,80,128]{2,1,0:T(8,128)(2,1)S(1)} %shard_map.98), channel_id=1, replica_groups=mesh['yl'=2,'x'=4,'z'=8,'yh'=2,'c'=2] {'z'}, dimensions={0} | all-to-all | bytes 327680 | tf_op jit(solution)/shard_map/all_to_all | solution.py:379
  70.7 0.9 shard_map.99
  71.6 5.7 %all-to-all-start.3 = ((bf16[32,80,128]{2,1,0:T(8,128)(2,1)}), bf16[32,80,128]{2,1,0:T(8,128)(2,1)S(1)}, u32[]{:S(2)}, u32[]{:S(2)}) async-start(bf16[32,80,128]{2,1,0:T(8,128)(2,1)} %shard_map.99), calls=%async_computation.3 | async-start | bytes 1310720 | tf_op jit(solution)/shard_map/all_to_all | solution.py:379
  77.3 6.3 %shard_map.95 = (f32[1536,128]{1,0:T(8,128)}, f32[1536,128]{1,0:T(8,128)}, bf16[1536,128]{1,0:T(8,128)(2,1)}, bf16[1536,128]{1,0:T(8,128)(2,1)}) custom-call(bf16[3200,128]{1,0:T(8,128)(2,1)} %get-tuple-element.24.g0_ref.refs_4_, bf16[3200,128]{1,0:T(8,128)(2,1)} %get-tuple-element.25.g1_ref.refs_5_, bf16[576,256]{1,0:T(8,128)(2,1)} %get-tuple-element.26.d_ref), custom_call_target="tpu_custom_call" | custom-call | flops 12884901888 | bytes 8388608 | tf_op jit(solution)/shard_map/pallas_call | solution.py:500
  83.5 0.4 collective-permute-start.2
  84.0 4.8 %collective-permute-start.3 = (bf16[1536,128]{1,0:T(8,128)(2,1)}, bf16[1536,128]{1,0:T(8,128)(2,1)S(1)}, u32[]{:S(2)}, u32[]{:S(2)}) collective-permute-start(bf16[1536,128]{1,0:T(8,128)(2,1)} %get-tuple-element.30), channel_id=1, source_target_pairs={{1,2},{3,4},{5,6},{7,8},{9,10},{11,12},{13,14},{15,16},{17,18},{19... | collective-permute-start | bytes 1179656 | tf_op jit(solution)/shard_map/ppermute | solution.py:395
  88.8 0.0 collective-permute-done.2.inner_ref
  88.8 9.2 %collective-permute-done.3.outer_ref = bf16[1536,128]{1,0:T(8,128)(2,1)S(1)} collective-permute-done((bf16[1536,128]{1,0:T(8,128)(2,1)}, bf16[1536,128]{1,0:T(8,128)(2,1)S(1)}, u32[]{:S(2)}, u32[]{:S(2)}) %collective-permute-start.3) | collective-permute-done | bytes 393248 | tf_op jit(solution)/shard_map/ppermute | solution.py:395
  98.0 2.9 %shard_map.96 = bf16[32,2,48,128]{3,2,1,0:T(8,128)(2,1)} custom-call(f32[1536,128]{1,0:T(8,128)} %get-tuple-element.27.own0_ref, f32[1536,128]{1,0:T(8,128)} %get-tuple-element.28.own1_ref, bf16[1536,128]{1,0:T(8,128)(2,1)S(1)} %collective-permute-done.2.inner_ref, bf16[1536,128]{1,0:T(8,128)(2,1)S(1)} %collective-permute-done.3.outer_ref), custom_call_target="tpu_custom_call" | custom-call | flops 268435456 | bytes 4194304 | tf_op jit(solution)/shard_map/pallas_call | solution.py:506
  101.0 0.0 all-to-all-done.3.in_ref
  101.0 1.2 %shard_map.100 = (f32[2048,128]{1,0:T(8,128)}, f32[9,3,32,64]{3,2,1,0:T(8,128)}, f32[1,64]{1,0:T(1,128)}) custom-call(bf16[32,80,128]{2,1,0:T(8,128)(2,1)S(1)} %all-to-all-done.3.in_ref), custom_call_target="tpu_custom_call" | custom-call | flops 4194304 | bytes 3145728 | tf_op jit(solution)/shard_map/pallas_call | solution.py:507
Async XLA Ops:
  0.6 18.0 %copy-start = (f32[64]{0:T(128)S(1)}, f32[64]{0:T(128)}, u32[]{:S(2)}) copy-start(f32[64]{0:T(128)} %refs_5_.1) | copy-start | bytes 772
  2.8 15.8 %collective-permute-start = (bf16[1600,128]{1,0:T(8,128)(2,1)}, bf16[1600,128]{1,0:T(8,128)(2,1)S(1)}, u32[]{:S(2)}, u32[]{:S(2)}) collective-permute-start(bf16[1600,128]{1,0:T(8,128)(2,1)} %get-tuple-element.20.refs_2_), channel_id=1, source_target_pairs={{0,1},{1,0},{2,3},{3,2},{4,5},{5,4},{6,7},{7,6},{8,9},{9,8},{10,11... | collective-permute-start | bytes 1228808 | tf_op jit(solution)/shard_map/ppermute | solution.py:395
  6.1 12.6 %collective-permute-start.1 = (bf16[1600,128]{1,0:T(8,128)(2,1)}, bf16[1600,128]{1,0:T(8,128)(2,1)S(1)}, u32[]{:S(2)}, u32[]{:S(2)}) collective-permute-start(bf16[1600,128]{1,0:T(8,128)(2,1)} %get-tuple-element.21.refs_3_), channel_id=1, source_target_pairs={{1,2},{3,4},{5,6},{7,8},{9,10},{11,12},{13,14},{15,16},{17,18},{19... | collective-permute-start | bytes 1228808 | tf_op jit(solution)/shard_map/ppermute | solution.py:395
  12.1 24.1 %all-to-all-start = ((bf16[32,64,128]{2,1,0:T(8,128)(2,1)}), bf16[32,64,128]{2,1,0:T(8,128)(2,1)S(1)}, u32[]{:S(2)}, u32[]{:S(2)}) async-start(bf16[32,64,128]{2,1,0:T(8,128)(2,1)} %get-tuple-element.31), calls=%async_computation | async-start | bytes 1048576 | tf_op jit(solution)/shard_map/all_to_all | solution.py:379
  71.6 29.4 %all-to-all-start.3 = ((bf16[32,80,128]{2,1,0:T(8,128)(2,1)}), bf16[32,80,128]{2,1,0:T(8,128)(2,1)S(1)}, u32[]{:S(2)}, u32[]{:S(2)}) async-start(bf16[32,80,128]{2,1,0:T(8,128)(2,1)} %shard_map.99), calls=%async_computation.3 | async-start | bytes 1310720 | tf_op jit(solution)/shard_map/all_to_all | solution.py:379
  83.5 5.3 %collective-permute-start.2 = (bf16[1536,128]{1,0:T(8,128)(2,1)}, bf16[1536,128]{1,0:T(8,128)(2,1)S(1)}, u32[]{:S(2)}, u32[]{:S(2)}) collective-permute-start(bf16[1536,128]{1,0:T(8,128)(2,1)} %get-tuple-element.29), channel_id=1, source_target_pairs={{0,1},{1,0},{2,3},{3,2},{4,5},{5,4},{6,7},{7,6},{8,9},{9,8},{10,11... | collective-permute-start | bytes 1179656 | tf_op jit(solution)/shard_map/ppermute | solution.py:395
  84.0 14.0 %collective-permute-start.3 = (bf16[1536,128]{1,0:T(8,128)(2,1)}, bf16[1536,128]{1,0:T(8,128)(2,1)S(1)}, u32[]{:S(2)}, u32[]{:S(2)}) collective-permute-start(bf16[1536,128]{1,0:T(8,128)(2,1)} %get-tuple-element.30), channel_id=1, source_target_pairs={{1,2},{3,4},{5,6},{7,8},{9,10},{11,12},{13,14},{15,16},{17,18},{19... | collective-permute-start | bytes 1179656 | tf_op jit(solution)/shard_map/ppermute | solution.py:395

commit v3 on v2

--- a/solution.py
+++ b/solution.py
@@ -108,8 +108,12 @@
     return ((far_outer, far_inner), (outer, inner), (inner, outer), (far_inner, far_outer))
 
 
+def g_sources(inner, outer):
+    return ((outer, inner), (inner, outer))
+
+
 def forward_kernel(*refs):
-    p_refs, (a_ref, bias_ref, cot_ref, act_ref, g0_ref, g1_ref) = refs[:4], refs[4:10]
+    p_refs, (a_ref, bias_ref, cot_ref, act_ref, inner_ref, outer_ref) = refs[:4], refs[4:10]
     planes, (a, cot, act, g0, g1, s0, s1, in_sem, act_sem) = refs[10:14], refs[14:]
     a_copy = pltpu.make_async_copy(a_ref, a, in_sem.at[8])
     a_copy.start()
@@ -167,7 +171,7 @@
     for n in range(8):
         some = pl.ds(8 * n, 8)
         outs.append(pltpu.make_async_copy(act.at[some], act_ref.at[some], act_sem.at[n]))
-    for n, (g_ref, g, s) in enumerate(((g0_ref, g0, s0), (g1_ref, g1, s1))):
+    for n, (g, s) in enumerate(((g0, s0), (g1, s1))):
 
         def rows_of(t, _, g=g, s=s):
             for y in range(8):
@@ -177,8 +181,8 @@
             return 0
 
         lax.fori_loop(0, NY // 8, rows_of, 0)
-        outs.append(pltpu.make_async_copy(g, g_ref, act_sem.at[8 + n]))
-        outs[-1].start()
+        first, second = (outer_ref, inner_ref) if n == 0 else (inner_ref, outer_ref)
+        outs += by_core([((g, first), (g, second))], act_sem.at[pl.ds(8 + n, 1)])
     for out in outs:
         out.wait()
 
@@ -187,7 +191,7 @@
     p_refs, g_refs, out_ref = refs[:4], refs[4:6], refs[6]
     planes, gs_buf, acc, sems = refs[7:11], refs[11:13], refs[13], refs[14]
     first, second = halves(x_sources(*p_refs), planes, CI, sems)
-    g_first, g_second = halves([(g, g) for g in g_refs], gs_buf, CO, sems.at[pl.ds(8, 4)])
+    g_first, g_second = halves(g_sources(*g_refs), gs_buf, CO, sems.at[pl.ds(8, 4)])
     acc[...] = jnp.zeros_like(acc)
     lane = lax.broadcasted_iota(jnp.int32, (CO, NX), 1)
 
@@ -229,32 +233,32 @@
     out_ref[464:512, :] = jnp.zeros((48, NX), BF)
 
 
-def back_kernel(g0_ref, g1_ref, d_ref, own0_ref, own1_ref, inner_ref, outer_ref, *rest):
-    g0, g1, d, s0, s1, low, high, sems, out_sem = rest
+def add_rows(s, q, z_rows, fresh):
+    for h in range(2):
+        rr = z_rows[:, NX * h : NX * (h + 1)]
+        y = shifted_sum(rr[128:192], rr[64:128], rr[0:64])
+        for p in range(2):
+            for m in range(4):
+                at = pl.ds(row_of(4 * q + 2 * h + p, m, 4), 8)
+                part = y[32 * p + 8 * m : 32 * p + 8 * m + 8]
+                s[at, :] = part if fresh else s[at, :] + part
+
+
+def window(g, q):
+    sides = [g[pl.ds(pl.multiple_of((2 * q + h) * (2 * CO), 2 * CO), 4 * CO), :] for h in range(2)]
+    return jnp.concatenate(sides, axis=1)
+
+
+def back_kernel(inner_ref, outer_ref, d_ref, own0_ref, own1_ref, g0, g1, d, s0, s1, sems, out_sem):
     d_copy = pltpu.make_async_copy(d_ref, d, sems.at[4])
     d_copy.start()
-    first, second = halves([(g0_ref, g0_ref), (g1_ref, g1_ref)], (g0, g1), CO, sems)
+    first, second = halves(g_sources(inner_ref, outer_ref), (g0, g1), CO, sems)
 
     def conv(q, _):
-        r = []
-        for g in (g0, g1):
-            sides = [
-                g[pl.ds(pl.multiple_of((2 * q + h) * (2 * CO), 2 * CO), 4 * CO), :] for h in range(2)
-            ]
-            r.append(jnp.dot(d[...], jnp.concatenate(sides, axis=1), preferred_element_type=F32))
-        volumes = (r[0][0:192], r[0][192:384] + r[1][0:192], r[0][384:576] + r[1][192:384], r[1][384:576])
-        for v, s in zip(volumes, (low, s0, s1, high)):
-            for h in range(2):
-                rr = v[:, NX * h : NX * (h + 1)]
-                y = shifted_sum(rr[128:192], rr[64:128], rr[0:64])
-                if s.dtype == BF:
-                    at = pl.multiple_of((2 * q + h) * (2 * CI), 2 * CI)
-                    s[pl.ds(at, 2 * CI), :] = y.astype(BF)
-                    continue
-                for p in range(2):
-                    for m in range(4):
-                        at = row_of(4 * q + 2 * h + p, m, 4)
-                        s[pl.ds(at, 8), :] = y[32 * p + 8 * m : 32 * p + 8 * m + 8]
+        r = jnp.dot(d[192:576, :], window(g0, q), preferred_element_type=F32)
+        r += jnp.dot(d[0:384, :], window(g1, q), preferred_element_type=F32)
+        add_rows(s0, q, r[0:192], True)
+        add_rows(s1, q, r[192:384], True)
         return 0
 
     d_copy.wait()
@@ -262,37 +266,34 @@
         for copy in part:
             copy.wait()
         lax.fori_loop(lo, lo + 6, conv, 0, unroll=2)
-    outs = by_core(
-        [((high, inner_ref), (low, inner_ref)), ((low, outer_ref), (high, outer_ref))],
-        out_sem.at[pl.ds(0, 2)],
-    )
+    outs = []
     for n, (s, own) in enumerate(((s0, own0_ref), (s1, own1_ref))):
-        outs.append(pltpu.make_async_copy(s, own, out_sem.at[2 + n]))
+        outs.append(pltpu.make_async_copy(s, own, out_sem.at[n]))
         outs[-1].start()
     for out in outs:
         out.wait()
 
 
-def finish_kernel(own0_ref, own1_ref, inner_ref, outer_ref, out_ref, s0, s1, e0, e1, buf, sems, out_sem):
-    loads = by_core(
-        [((outer_ref, e0), (inner_ref, e0)), ((inner_ref, e1), (outer_ref, e1))], sems.at[pl.ds(0, 2)]
-    )
+def finish_kernel(own0_ref, own1_ref, inner_ref, outer_ref, d_ref, out_ref, *rest):
+    s0, s1, low, high, d, buf, sems, out_sem = rest
+    first, second = halves(g_sources(inner_ref, outer_ref), (low, high), CO, sems)
+    first.append(pltpu.make_async_copy(d_ref, d, sems.at[4]))
+    first[-1].start()
     for n, (own, s) in enumerate(((own0_ref, s0), (own1_ref, s1))):
-        loads.append(pltpu.make_async_copy(own, s, sems.at[2 + n]))
-        loads[-1].start()
-    for load in loads:
-        load.wait()
-
-    def add(t, _):
-        for s, e in ((s0, e0), (s1, e1)):
-            for y in range(8):
-                v = e[pl.ds(pl.multiple_of((t * 8 + y) * CI, CI), CI), :].astype(F32)
-                for m in range(4):
-                    at = pl.ds((t * 4 + m) * 64 + y * 8, 8)
-                    s[at, :] += v[8 * m : 8 * m + 8]
+        first.append(pltpu.make_async_copy(own, s, sems.at[5 + n]))
+        first[-1].start()
+
+    def conv(q, _):
+        r0 = jnp.dot(d[384:576, :], window(low, q), preferred_element_type=F32)
+        r1 = jnp.dot(d[0:192, :], window(high, q), preferred_element_type=F32)
+        add_rows(s0, q, r0, False)
+        add_rows(s1, q, r1, False)
         return 0
 
-    lax.fori_loop(0, NY // 8, add, 0)
+    for part, lo in ((first, 0), (second, 6)):
+        for copy in part:
+            copy.wait()
+        lax.fori_loop(lo, lo + 6, conv, 0, unroll=2)
 
     def gather(m, _):
         for n in range(8):
@@ -441,28 +442,25 @@
         5 << 20,
     )
     edge = (NY * CI, NX)
+    dbuf = pltpu.VMEM((576, 256), BF)
     back = call(
         back_kernel,
-        (pltpu.HBM(edge, F32), pltpu.HBM(edge, F32), pltpu.HBM(edge, BF), pltpu.HBM(edge, BF)),
-        [gbuf] * 2
-        + [pltpu.VMEM((576, 256), BF)]
-        + [pltpu.VMEM(edge, F32)] * 2
-        + [pltpu.VMEM(edge, BF)] * 2
-        + [DMA((5,)), DMA((4,))],
+        (pltpu.HBM(edge, F32), pltpu.HBM(edge, F32)),
+        [gbuf] * 2 + [dbuf] + [pltpu.VMEM(edge, F32)] * 2 + [DMA((5,)), DMA((2,))],
         [HBM] * 3,
-        3 << 32,
-        8 << 20,
-        (HBM,) * 4,
+        2 << 32,
+        6 << 20,
+        (HBM,) * 2,
     )
     finish = call(
         finish_kernel,
         pltpu.HBM((CI, 2, NY, NX), BF),
         [pltpu.VMEM(edge, F32)] * 2
-        + [pltpu.VMEM(edge, BF)] * 2
-        + [pltpu.VMEM((CI, 2, NY, NX), BF), DMA((4,)), DMA((4,))],
-        [HBM, HBM, ANY, ANY],
-        1 << 28,
-        4 << 20,
+        + [gbuf] * 2
+        + [dbuf, pltpu.VMEM((CI, 2, NY, NX), BF), DMA((7,)), DMA((4,))],
+        [HBM, HBM, ANY, ANY, HBM],
+        1 << 32,
+        6 << 20,
         HBM,
     )
     prep = call(
@@ -494,16 +492,16 @@
     wf, wb, fin = prep(far(kernel.transpose(0, 1, 2, 4, 3)), far(finished_grads.reshape(2048, NX)))
     fin = exchange(fin, PLANE)
     x = (far_inner, far_outer, far(inner), far(outer))
-    act, g0, g1 = forward(*x, far(wf), bias, far(cotangent[0]))
-    taps = weight(*x, far(g0), far(g1))
+    act, inner, outer = forward(*x, far(wf), bias, far(cotangent[0]))
+    far_inner, far_outer = swap(inner, outer)
+    taps = weight(*x, far(inner), far(outer))
     taps = exchange(taps.reshape(CHUNKS, TROWS, NX), PLANE)
-    own0, own1, inner, outer = back(far(g0), far(g1), far(wb))
-    far_inner, far_outer = swap(inner, outer)
+    own0, own1 = back(far(inner), far(outer), far(wb))
     joined = join_b(fin, taps)
     joined = exchange(joined, COLUMN)
     joined = join_c(joined)
     joined = exchange(joined, PLANE)
-    grad_volumes = finish(far(own0), far(own1), far_inner, far_outer)
+    grad_volumes = finish(far(own0), far(own1), far_inner, far_outer, far(wb))
     summed, grad_taps, grad_bias = out(joined)
     grad_kernel = grad_taps.reshape(3, 3, 3, CI, CO).transpose(0, 1, 2, 4, 3)
     return act[None], grad_volumes[None], grad_kernel, grad_bias.reshape(CO), summed.reshape(-1)

time: 103 us -> 101 us (0.981)
  the two profiles are of different devices: /device:TPU:1 before, /device:TPU:33 now
where the time goes in v3:
time: 101 us; the launch traced here: 100 us
  Pallas kernels  36.4 us (36%)
  starting transfers between devices  32.3 us (32%)
  waiting for transfers between devices  16.4 us (16%)
  blocking collectives  14.4 us (14%)
    all_to_all x3, starting transfers between devices, exchange(): return lax.all_to_all(parts, axes, 0, 0)  22.8 us
    all_to_all x1, blocking collectives, exchange(): return lax.all_to_all(parts, axes, 0, 0)  14.4 us
    ppermute x2, waiting for transfers between devices, swap(): lax.ppermute(outer, SPACE, off_chip)  13.4 us
    pallas_call x1, Pallas kernels, layer(): act, inner, outer = forward(*x, far(wf), bias, far(cotangent[0]))  9.96 us
    ppermute x2, starting transfers between devices, swap(): lax.ppermute(outer, SPACE, off_chip)  7.82 us
    pallas_call x1, Pallas kernels, layer(): taps = weight(*x, far(inner), far(outer))  7.52 us
    pallas_call x1, Pallas kernels, layer(): grad_volumes = finish(far(own0), far(own1), far_inner, far_outer, far(wb))  5.63 us
    pallas_call x1, Pallas kernels, layer(): own0, own1 = back(far(inner), far(outer), far(wb))  5.24 us
  transfers between devices with their start and end apart: 7, of which 3 were waited for; matrix products, arithmetic and copies ran while one was open for 0% of the time, Pallas kernels for 32%

profile of v3, /device:TPU:33, one launch (start us, length us, event | category | flops | bytes accessed | tf_op | source)
XLA Modules:
  0.0 100.3 jit_solution(1776901751182488748)
XLA Ops:
  0.6 0.0 copy-start
  0.6 2.2 %shard_map.92 = (bf16[1600,128]{1,0:T(8,128)(2,1)}, bf16[1600,128]{1,0:T(8,128)(2,1)}) custom-call(bf16[32,2,48,128]{3,2,1,0:T(8,128)(2,1)} %bitcast.14), custom_call_target="tpu_custom_call" | custom-call | flops 4194304 | bytes 3145728 | tf_op jit(solution)/shard_map/pallas_call | solution.py:490
  2.8 0.8 collective-permute-start
  3.6 4.7 %collective-permute-start.1 = (bf16[1600,128]{1,0:T(8,128)(2,1)}, bf16[1600,128]{1,0:T(8,128)(2,1)S(1)}, u32[]{:S(2)}, u32[]{:S(2)}) collective-permute-start(bf16[1600,128]{1,0:T(8,128)(2,1)} %get-tuple-element.19.refs_3_), channel_id=1, source_target_pairs={{1,2},{3,4},{5,6},{7,8},{9,10},{11,12},{13,14},{15,16},{17,18},{19... | collective-permute-start | bytes 1228808 | tf_op jit(solution)/shard_map/ppermute | solution.py:396
  8.3 3.0 %shard_map.93 = (bf16[768,512]{1,0:T(8,128)(2,1)}, bf16[576,256]{1,0:T(8,128)(2,1)}, bf16[32,64,128]{2,1,0:T(8,128)(2,1)}) custom-call(bf16[3,3,3,32,64]{4,3,2,1,0:T(8,128)(2,1)} %bitcast.15, f32[2048,128]{1,0:T(8,128)} %bitcast.13), custom_call_target="tpu_custom_call" | custom-call | flops 4194304 | bytes 3145728 | tf_op jit(solution)/shard_map/pallas_call | solution.py:492
  11.3 6.4 %all-to-all-start = ((bf16[32,64,128]{2,1,0:T(8,128)(2,1)}), bf16[32,64,128]{2,1,0:T(8,128)(2,1)S(1)}, u32[]{:S(2)}, u32[]{:S(2)}) async-start(bf16[32,64,128]{2,1,0:T(8,128)(2,1)} %get-tuple-element.27), calls=%async_computation | async-start | bytes 1048576 | tf_op jit(solution)/shard_map/all_to_all | solution.py:380
  17.7 0.0 collective-permute-done.refs_0_
  17.7 1.2 %collective-permute-done.1.refs_1_ = bf16[1600,128]{1,0:T(8,128)(2,1)S(1)} collective-permute-done((bf16[1600,128]{1,0:T(8,128)(2,1)}, bf16[1600,128]{1,0:T(8,128)(2,1)S(1)}, u32[]{:S(2)}, u32[]{:S(2)}) %collective-permute-start.1) | collective-permute-done | bytes 409632 | tf_op jit(solution)/shard_map/ppermute | solution.py:396
  18.9 0.0 copy-done
  18.9 10.0 %shard_map.94 = (bf16[64,2,48,128]{3,2,1,0:T(8,128)(2,1)}, bf16[3200,128]{1,0:T(8,128)(2,1)}, bf16[3200,128]{1,0:T(8,128)(2,1)}) custom-call(bf16[1600,128]{1,0:T(8,128)(2,1)S(1)} %collective-permute-done.refs_0_, bf16[1600,128]{1,0:T(8,128)(2,1)S(1)} %collective-permute-done.1.refs_1_, bf16[1600,128]{1,0:T(8,128)(2,1)} %get-tuple-element.18.refs_2_, ...), custom_call_target="tpu_custom_call" | custom-call | flops 12884901888 | bytes 8388608 | tf_op jit(solution)/shard_map/pallas_call | solution.py:495
  28.9 0.0 copy-start.1
  28.9 7.5 %shard_map.97 = bf16[512,128]{1,0:T(8,128)(2,1)S(1)} custom-call(bf16[1600,128]{1,0:T(8,128)(2,1)S(1)} %collective-permute-done.refs_0_, bf16[1600,128]{1,0:T(8,128)(2,1)S(1)} %collective-permute-done.1.refs_1_, bf16[1600,128]{1,0:T(8,128)(2,1)} %get-tuple-element.18.refs_2_, bf16[1600,128]{1,0:T(8,128)(2,1)} %get-tuple-element.19.refs_3_, ...), custom_call_target="tpu_custom_call" | custom-call | flops 12884901888 | bytes 5242880 | tf_op jit(solution)/shard_map/pallas_call | solution.py:497
  36.4 0.0 all-to-all-done.f_ref
  36.4 14.4 %all_to_all.20.t_ref = bf16[32,16,128]{2,1,0:T(8,128)(2,1)S(1)} all-to-all(bf16[32,16,128]{2,1,0:T(8,128)(2,1)S(1)} %bitcast.12), channel_id=1, replica_groups=mesh['yl'=2,'x'=4,'z'=8,'yh'=2,'c'=2] {'yl','x','yh','c'}, dimensions={0} | all-to-all | bytes 262144 | tf_op jit(solution)/shard_map/all_to_all | solution.py:380
  50.9 0.8 shard_map.98
  51.6 10.3 %all-to-all-start.2 = ((bf16[8,80,128]{2,1,0:T(8,128)(2,1)}), bf16[8,80,128]{2,1,0:T(8,128)(2,1)S(1)}, u32[]{:S(2)}, u32[]{:S(2)}) async-start(bf16[8,80,128]{2,1,0:T(8,128)(2,1)} %shard_map.98), calls=%async_computation.2 | async-start | bytes 327680 | tf_op jit(solution)/shard_map/all_to_all | solution.py:380
  61.9 1.0 collective-permute-start.2
  62.9 0.0 copy-done.1
  62.9 3.1 %collective-permute-start.3 = (bf16[3200,128]{1,0:T(8,128)(2,1)S(1)}, bf16[3200,128]{1,0:T(8,128)(2,1)S(1)}, u32[]{:S(2)}, u32[]{:S(2)}) collective-permute-start(bf16[3200,128]{1,0:T(8,128)(2,1)S(1)} %copy-done.1), channel_id=1, source_target_pairs={{1,2},{3,4},{5,6},{7,8},{9,10},{11,12},{13,14},{15,16},{17,18},{19... | collective-permute-start | bytes 2457608 | tf_op jit(solution)/shard_map/ppermute | solution.py:396
  66.0 3.0 %all-to-all-done.2.in_ref = bf16[8,80,128]{2,1,0:T(8,128)(2,1)S(1)} async-done(((bf16[8,80,128]{2,1,0:T(8,128)(2,1)}), bf16[8,80,128]{2,1,0:T(8,128)(2,1)S(1)}, u32[]{:S(2)}, u32[]{:S(2)}) %all-to-all-start.2) | async-done | bytes 163872 | tf_op jit(solution)/shard_map/all_to_all | solution.py:380
  69.0 0.9 shard_map.99
  69.9 6.0 %all-to-all-start.3 = ((bf16[32,80,128]{2,1,0:T(8,128)(2,1)}), bf16[32,80,128]{2,1,0:T(8,128)(2,1)S(1)}, u32[]{:S(2)}, u32[]{:S(2)}) async-start(bf16[32,80,128]{2,1,0:T(8,128)(2,1)} %shard_map.99), calls=%async_computation.3 | async-start | bytes 1310720 | tf_op jit(solution)/shard_map/all_to_all | solution.py:380
  75.9 5.2 %shard_map.95 = (f32[1536,128]{1,0:T(8,128)}, f32[1536,128]{1,0:T(8,128)}) custom-call(bf16[3200,128]{1,0:T(8,128)(2,1)} %get-tuple-element.22.inner_ref.refs_4_, bf16[3200,128]{1,0:T(8,128)(2,1)} %get-tuple-element.23.outer_ref.refs_5_, bf16[576,256]{1,0:T(8,128)(2,1)} %get-tuple-element.24.d_ref), custom_call_target="tpu_custom_call" | custom-call | flops 8589934592 | bytes 6291456 | tf_op jit(solution)/shard_map/pallas_call | solution.py:499
  81.2 0.0 collective-permute-done.2.inner_ref
  81.2 12.2 %collective-permute-done.3.outer_ref = bf16[3200,128]{1,0:T(8,128)(2,1)S(1)} collective-permute-done((bf16[3200,128]{1,0:T(8,128)(2,1)S(1)}, bf16[3200,128]{1,0:T(8,128)(2,1)S(1)}, u32[]{:S(2)}, u32[]{:S(2)}) %collective-permute-start.3) | collective-permute-done | bytes 819232 | tf_op jit(solution)/shard_map/ppermute | solution.py:396
  93.4 5.6 %shard_map.96 = bf16[32,2,48,128]{3,2,1,0:T(8,128)(2,1)} custom-call(f32[1536,128]{1,0:T(8,128)} %get-tuple-element.25.own0_ref, f32[1536,128]{1,0:T(8,128)} %get-tuple-element.26.own1_ref, bf16[3200,128]{1,0:T(8,128)(2,1)S(1)} %collective-permute-done.2.inner_ref, bf16[3200,128]{1,0:T(8,128)(2,1)S(1)} %collective-permute-done.3.outer_ref, ...), custom_call_target="tpu_custom_call" | custom-call | flops 4294967296 | bytes 6291456 | tf_op jit(solution)/shard_map/pallas_call | solution.py:504
  99.1 0.0 all-to-all-done.3.in_ref
  99.1 1.2 %shard_map.100 = (f32[2048,128]{1,0:T(8,128)}, f32[9,3,32,64]{3,2,1,0:T(8,128)}, f32[1,64]{1,0:T(1,128)}) custom-call(bf16[32,80,128]{2,1,0:T(8,128)(2,1)S(1)} %all-to-all-done.3.in_ref), custom_call_target="tpu_custom_call" | custom-call | flops 4194304 | bytes 3145728 | tf_op jit(solution)/shard_map/pallas_call | solution.py:505
Async XLA Ops:
  0.6 18.3 %copy-start = (f32[64]{0:T(128)S(1)}, f32[64]{0:T(128)}, u32[]{:S(2)}) copy-start(f32[64]{0:T(128)} %refs_5_.1) | copy-start | bytes 772
  2.8 14.9 %collective-permute-start = (bf16[1600,128]{1,0:T(8,128)(2,1)}, bf16[1600,128]{1,0:T(8,128)(2,1)S(1)}, u32[]{:S(2)}, u32[]{:S(2)}) collective-permute-start(bf16[1600,128]{1,0:T(8,128)(2,1)} %get-tuple-element.18.refs_2_), channel_id=1, source_target_pairs={{0,1},{1,0},{2,3},{3,2},{4,5},{5,4},{6,7},{7,6},{8,9},{9,8},{10,11... | collective-permute-start | bytes 1228808 | tf_op jit(solution)/shard_map/ppermute | solution.py:396
  3.6 15.4 %collective-permute-start.1 = (bf16[1600,128]{1,0:T(8,128)(2,1)}, bf16[1600,128]{1,0:T(8,128)(2,1)S(1)}, u32[]{:S(2)}, u32[]{:S(2)}) collective-permute-start(bf16[1600,128]{1,0:T(8,128)(2,1)} %get-tuple-element.19.refs_3_), channel_id=1, source_target_pairs={{1,2},{3,4},{5,6},{7,8},{9,10},{11,12},{13,14},{15,16},{17,18},{19... | collective-permute-start | bytes 1228808 | tf_op jit(solution)/shard_map/ppermute | solution.py:396
  11.3 25.1 %all-to-all-start = ((bf16[32,64,128]{2,1,0:T(8,128)(2,1)}), bf16[32,64,128]{2,1,0:T(8,128)(2,1)S(1)}, u32[]{:S(2)}, u32[]{:S(2)}) async-start(bf16[32,64,128]{2,1,0:T(8,128)(2,1)} %get-tuple-element.27), calls=%async_computation | async-start | bytes 1048576 | tf_op jit(solution)/shard_map/all_to_all | solution.py:380
  28.9 34.0 %copy-start.1 = (bf16[3200,128]{1,0:T(8,128)(2,1)S(1)}, bf16[3200,128]{1,0:T(8,128)(2,1)}, u32[]{:S(2)}) copy-start(bf16[3200,128]{1,0:T(8,128)(2,1)} %get-tuple-element.23.outer_ref.refs_5_) | copy-start | bytes 2457604
  51.6 17.4 %all-to-all-start.2 = ((bf16[8,80,128]{2,1,0:T(8,128)(2,1)}), bf16[8,80,128]{2,1,0:T(8,128)(2,1)S(1)}, u32[]{:S(2)}, u32[]{:S(2)}) async-start(bf16[8,80,128]{2,1,0:T(8,128)(2,1)} %shard_map.98), calls=%async_computation.2 | async-start | bytes 327680 | tf_op jit(solution)/shard_map/all_to_all | solution.py:380
  61.9 19.3 %collective-permute-start.2 = (bf16[3200,128]{1,0:T(8,128)(2,1)}, bf16[3200,128]{1,0:T(8,128)(2,1)S(1)}, u32[]{:S(2)}, u32[]{:S(2)}) collective-permute-start(bf16[3200,128]{1,0:T(8,128)(2,1)} %get-tuple-element.22.inner_ref.refs_4_), channel_id=1, source_target_pairs={{0,1},{1,0},{2,3},{3,2},{4,5},{5,4},{6,7},{7,6},{8,9},{9,8},{10,11... | collective-permute-start | bytes 2457608 | tf_op jit(solution)/shard_map/ppermute | solution.py:396
  62.9 30.5 %collective-permute-start.3 = (bf16[3200,128]{1,0:T(8,128)(2,1)S(1)}, bf16[3200,128]{1,0:T(8,128)(2,1)S(1)}, u32[]{:S(2)}, u32[]{:S(2)}) collective-permute-start(bf16[3200,128]{1,0:T(8,128)(2,1)S(1)} %copy-done.1), channel_id=1, source_target_pairs={{1,2},{3,4},{5,6},{7,8},{9,10},{11,12},{13,14},{15,16},{17,18},{19... | collective-permute-start | bytes 2457608 | tf_op jit(solution)/shard_map/ppermute | solution.py:396
  69.9 29.2 %all-to-all-start.3 = ((bf16[32,80,128]{2,1,0:T(8,128)(2,1)}), bf16[32,80,128]{2,1,0:T(8,128)(2,1)S(1)}, u32[]{:S(2)}, u32[]{:S(2)}) async-start(bf16[32,80,128]{2,1,0:T(8,128)(2,1)} %shard_map.99), calls=%async_computation.3 | async-start | bytes 1310720 | tf_op jit(solution)/shard_map/all_to_all | solution.py:380

commit v4 on v3

--- a/solution.py
+++ b/solution.py
@@ -11,11 +11,11 @@
 F32 = jnp.float32
 CI, CO, NY, NX = 32, 64, 48, 128
 PADY = NY + 2
-PLANE = ("yl", "x", "yh", "c")
-COLUMN = "z"
-CHUNKS, COLS = 32, 8
-FROWS, TROWS = 64, 16
-SPACE = ("z", "yh", "c")
+PLANE = ("yl", "x", "zl", "yh", "c")
+COLUMN = "zh"
+CHUNKS, COLS = 64, 4
+FROWS, TROWS = 2048 // CHUNKS, 512 // CHUNKS
+SPACE = ("zh", "zl", "yh", "c")
 
 
 def call(body, outs, scratch, specs, flops, nbytes, out_specs=None):
@@ -344,7 +344,8 @@
     for n, copy in enumerate(f_copies):
         copy.wait()
         part = f_ref[512 * n : 512 * n + 512, :]
-        out_ref[8 * n : 8 * n + 8] = part.reshape(8, FROWS, NX).astype(BF)
+        some = CHUNKS // 4
+        out_ref[some * n : some * n + some] = part.reshape(some, FROWS, NX).astype(BF)
     d_copy.wait()
     a_copy.wait()
 
@@ -508,7 +509,7 @@
 
 
 def solution(mesh):
-    fine = Mesh(mesh.devices.reshape(2, 4, 8, 2, 2), ("yl", "x", "z", "yh", "c"))
+    fine = Mesh(mesh.devices.reshape(2, 4, 4, 2, 2, 2), ("yl", "x") + SPACE)
     dp = ("yl", "x")
     slab = P(dp, None, SPACE, None, None)
     return jax.shard_map(

time: 101 us -> 128 us (1.27)
  the two profiles are of different devices: /device:TPU:33 before, /device:TPU:1 now
where the time goes in v4:
time: 128 us; the launch traced here: 126 us
  blocking collectives  48.8 us (38%)
  Pallas kernels  34.9 us (27%)
  waiting for transfers between devices  23.5 us (18%)
  starting transfers between devices  17.6 us (14%)
    all_to_all x3, blocking collectives, exchange(): return lax.all_to_all(parts, axes, 0, 0)  48.8 us
    ppermute x2, waiting for transfers between devices, swap(): lax.ppermute(outer, SPACE, off_chip)  23.4 us
    pallas_call x1, Pallas kernels, layer(): act, inner, outer = forward(*x, far(wf), bias, far(cotangent[0]))  9.98 us
    ppermute x2, starting transfers between devices, swap(): lax.ppermute(outer, SPACE, off_chip)  7.66 us
    pallas_call x1, Pallas kernels, layer(): taps = weight(*x, far(inner), far(outer))  7.53 us
    all_to_all x1, starting transfers between devices, exchange(): return lax.all_to_all(parts, axes, 0, 0)  6.06 us
    pallas_call x1, Pallas kernels, layer(): grad_volumes = finish(far(own0), far(own1), far_inner, far_outer, far(wb))  5.63 us
    pallas_call x1, Pallas kernels, layer(): own0, own1 = back(far(inner), far(outer), far(wb))  5.24 us
  transfers between devices with their start and end apart: 5, of which 2 were waited for; matrix products, arithmetic and copies ran while one was open for 0% of the time, Pallas kernels for 10%

profile of v4, /device:TPU:1, one launch (start us, length us, event | category | flops | bytes accessed | tf_op | source)
XLA Modules:
  0.0 125.5 jit_solution(2854352092606161974)
XLA Ops:
  0.6 0.0 copy-start
  0.6 2.2 %shard_map.92 = (bf16[1600,128]{1,0:T(8,128)(2,1)}, bf16[1600,128]{1,0:T(8,128)(2,1)}) custom-call(bf16[32,2,48,128]{3,2,1,0:T(8,128)(2,1)} %bitcast.14), custom_call_target="tpu_custom_call" | custom-call | flops 4194304 | bytes 3145728 | tf_op jit(solution)/shard_map/pallas_call | solution.py:491
  2.8 3.3 %collective-permute-start = (bf16[1600,128]{1,0:T(8,128)(2,1)}, bf16[1600,128]{1,0:T(8,128)(2,1)S(1)}, u32[]{:S(2)}, u32[]{:S(2)}) collective-permute-start(bf16[1600,128]{1,0:T(8,128)(2,1)} %get-tuple-element.18.refs_2_), channel_id=1, source_target_pairs={{0,1},{1,0},{2,3},{3,2},{4,5},{5,4},{6,7},{7,6},{8,9},{9,8},{10,11... | collective-permute-start | bytes 1228808 | tf_op jit(solution)/shard_map/ppermute | solution.py:397
  6.1 3.0 %collective-permute-start.1 = (bf16[1600,128]{1,0:T(8,128)(2,1)}, bf16[1600,128]{1,0:T(8,128)(2,1)S(1)}, u32[]{:S(2)}, u32[]{:S(2)}) collective-permute-start(bf16[1600,128]{1,0:T(8,128)(2,1)} %get-tuple-element.19.refs_3_), channel_id=1, source_target_pairs={{1,2},{3,4},{5,6},{7,8},{9,10},{11,12},{13,14},{15,16},{17,18},{19... | collective-permute-start | bytes 1228808 | tf_op jit(solution)/shard_map/ppermute | solution.py:397
  9.1 2.2 %shard_map.93 = (bf16[768,512]{1,0:T(8,128)(2,1)}, bf16[576,256]{1,0:T(8,128)(2,1)}, bf16[64,32,128]{2,1,0:T(8,128)(2,1)S(1)}) custom-call(bf16[3,3,3,32,64]{4,3,2,1,0:T(8,128)(2,1)} %bitcast.15, f32[2048,128]{1,0:T(8,128)} %bitcast.13), custom_call_target="tpu_custom_call" | custom-call | flops 4194304 | bytes 3145728 | tf_op jit(solution)/shard_map/pallas_call | solution.py:493
  11.3 0.0 collective-permute-done.refs_0_
  11.3 7.4 %collective-permute-done.1.refs_1_ = bf16[1600,128]{1,0:T(8,128)(2,1)S(1)} collective-permute-done((bf16[1600,128]{1,0:T(8,128)(2,1)}, bf16[1600,128]{1,0:T(8,128)(2,1)S(1)}, u32[]{:S(2)}, u32[]{:S(2)}) %collective-permute-start.1) | collective-permute-done | bytes 409632 | tf_op jit(solution)/shard_map/ppermute | solution.py:397
  18.7 0.0 copy-done
  18.7 10.0 %shard_map.94 = (bf16[64,2,48,128]{3,2,1,0:T(8,128)(2,1)}, bf16[3200,128]{1,0:T(8,128)(2,1)}, bf16[3200,128]{1,0:T(8,128)(2,1)}) custom-call(bf16[1600,128]{1,0:T(8,128)(2,1)S(1)} %collective-permute-done.refs_0_, bf16[1600,128]{1,0:T(8,128)(2,1)S(1)} %collective-permute-done.1.refs_1_, bf16[1600,128]{1,0:T(8,128)(2,1)} %get-tuple-element.18.refs_2_, ...), custom_call_target="tpu_custom_call" | custom-call | flops 12884901888 | bytes 8388608 | tf_op jit(solution)/shard_map/pallas_call | solution.py:496
  28.7 7.5 %shard_map.97 = bf16[512,128]{1,0:T(8,128)(2,1)S(1)} custom-call(bf16[1600,128]{1,0:T(8,128)(2,1)S(1)} %collective-permute-done.refs_0_, bf16[1600,128]{1,0:T(8,128)(2,1)S(1)} %collective-permute-done.1.refs_1_, bf16[1600,128]{1,0:T(8,128)(2,1)} %get-tuple-element.18.refs_2_, bf16[1600,128]{1,0:T(8,128)(2,1)} %get-tuple-element.19.refs_3_, ...), custom_call_target="tpu_custom_call" | custom-call | flops 12884901888 | bytes 5242880 | tf_op jit(solution)/shard_map/pallas_call | solution.py:498
  36.2 18.3 %all_to_all.20.t_ref = bf16[64,8,128]{2,1,0:T(8,128)(2,1)S(1)} all-to-all(bf16[64,8,128]{2,1,0:T(8,128)(2,1)S(1)} %bitcast.12), channel_id=1, replica_groups=mesh['yl'=2,'x'=4,'zh'=4,'zl'=2,'yh'=2,'c'=2] {'yl','x','zl','yh','c'}, dimensions={0} | all-to-all | bytes 262144 | tf_op jit(solution)/shard_map/all_to_all | solution.py:381
  54.5 16.5 %all_to_all.21.f_ref = bf16[64,32,128]{2,1,0:T(8,128)(2,1)S(1)} all-to-all(bf16[64,32,128]{2,1,0:T(8,128)(2,1)S(1)} %get-tuple-element.27), channel_id=1, replica_groups=mesh['yl'=2,'x'=4,'zh'=4,'zl'=2,'yh'=2,'c'=2] {'yl','x','zl','yh','c'}, dimensions={0} | all-to-all | bytes 1048576 | tf_op jit(solution)/shard_map/all_to_all | solution.py:381
  71.0 0.0 copy-start.2
  71.0 0.0 copy-start.1
  71.0 0.1 shard_map.98
  71.1 14.0 %all_to_all.22.in_ref = bf16[4,40,128]{2,1,0:T(8,128)(2,1)S(1)} all-to-all(bf16[4,40,128]{2,1,0:T(8,128)(2,1)S(1)} %shard_map.98), channel_id=1, replica_groups=mesh['yl'=2,'x'=4,'zh'=4,'zl'=2,'yh'=2,'c'=2] {'zh'}, dimensions={0} | all-to-all | bytes 81920 | tf_op jit(solution)/shard_map/all_to_all | solution.py:381
  85.1 0.9 shard_map.99
  86.0 6.1 %all-to-all-start.3 = ((bf16[64,40,128]{2,1,0:T(8,128)(2,1)}), bf16[64,40,128]{2,1,0:T(8,128)(2,1)S(1)}, u32[]{:S(2)}, u32[]{:S(2)}) async-start(bf16[64,40,128]{2,1,0:T(8,128)(2,1)} %shard_map.99), calls=%async_computation.3 | async-start | bytes 1310720 | tf_op jit(solution)/shard_map/all_to_all | solution.py:381
  92.0 0.0 copy-done.2
  92.1 0.6 collective-permute-start.2
  92.6 0.0 copy-done.1
  92.6 4.7 %collective-permute-start.3 = (bf16[3200,128]{1,0:T(8,128)(2,1)S(1)}, bf16[3200,128]{1,0:T(8,128)(2,1)S(1)}, u32[]{:S(2)}, u32[]{:S(2)}) collective-permute-start(bf16[3200,128]{1,0:T(8,128)(2,1)S(1)} %copy-done.1), channel_id=1, source_target_pairs={{1,2},{3,4},{5,6},{7,8},{9,10},{11,12},{13,14},{15,16},{17,18},{19... | collective-permute-start | bytes 2457608 | tf_op jit(solution)/shard_map/ppermute | solution.py:397
  97.3 5.2 %shard_map.95 = (f32[1536,128]{1,0:T(8,128)}, f32[1536,128]{1,0:T(8,128)}) custom-call(bf16[3200,128]{1,0:T(8,128)(2,1)} %get-tuple-element.22.inner_ref.refs_4_, bf16[3200,128]{1,0:T(8,128)(2,1)} %get-tuple-element.23.outer_ref.refs_5_, bf16[576,256]{1,0:T(8,128)(2,1)} %get-tuple-element.24.d_ref), custom_call_target="tpu_custom_call" | custom-call | flops 8589934592 | bytes 6291456 | tf_op jit(solution)/shard_map/pallas_call | solution.py:500
  102.6 0.0 collective-permute-done.2.inner_ref
  102.6 16.1 %collective-permute-done.3.outer_ref = bf16[3200,128]{1,0:T(8,128)(2,1)S(1)} collective-permute-done((bf16[3200,128]{1,0:T(8,128)(2,1)S(1)}, bf16[3200,128]{1,0:T(8,128)(2,1)S(1)}, u32[]{:S(2)}, u32[]{:S(2)}) %collective-permute-start.3) | collective-permute-done | bytes 819232 | tf_op jit(solution)/shard_map/ppermute | solution.py:397
  118.6 5.6 %shard_map.96 = bf16[32,2,48,128]{3,2,1,0:T(8,128)(2,1)} custom-call(f32[1536,128]{1,0:T(8,128)} %get-tuple-element.25.own0_ref, f32[1536,128]{1,0:T(8,128)} %get-tuple-element.26.own1_ref, bf16[3200,128]{1,0:T(8,128)(2,1)S(1)} %collective-permute-done.2.inner_ref, bf16[3200,128]{1,0:T(8,128)(2,1)S(1)} %collective-permute-done.3.outer_ref, ...), custom_call_target="tpu_custom_call" | custom-call | flops 4294967296 | bytes 6291456 | tf_op jit(solution)/shard_map/pallas_call | solution.py:505
  124.3 0.0 all-to-all-done.3.in_ref
  124.3 1.2 shard_map.100
Async XLA Ops:
  0.6 18.0 %copy-start = (f32[64]{0:T(128)S(1)}, f32[64]{0:T(128)}, u32[]{:S(2)}) copy-start(f32[64]{0:T(128)} %refs_5_.1) | copy-start | bytes 772
  2.8 8.5 %collective-permute-start = (bf16[1600,128]{1,0:T(8,128)(2,1)}, bf16[1600,128]{1,0:T(8,128)(2,1)S(1)}, u32[]{:S(2)}, u32[]{:S(2)}) collective-permute-start(bf16[1600,128]{1,0:T(8,128)(2,1)} %get-tuple-element.18.refs_2_), channel_id=1, source_target_pairs={{0,1},{1,0},{2,3},{3,2},{4,5},{5,4},{6,7},{7,6},{8,9},{9,8},{10,11... | collective-permute-start | bytes 1228808 | tf_op jit(solution)/shard_map/ppermute | solution.py:397
  6.1 12.6 %collective-permute-start.1 = (bf16[1600,128]{1,0:T(8,128)(2,1)}, bf16[1600,128]{1,0:T(8,128)(2,1)S(1)}, u32[]{:S(2)}, u32[]{:S(2)}) collective-permute-start(bf16[1600,128]{1,0:T(8,128)(2,1)} %get-tuple-element.19.refs_3_), channel_id=1, source_target_pairs={{1,2},{3,4},{5,6},{7,8},{9,10},{11,12},{13,14},{15,16},{17,18},{19... | collective-permute-start | bytes 1228808 | tf_op jit(solution)/shard_map/ppermute | solution.py:397
  71.0 21.1 %copy-start.2 = (bf16[3200,128]{1,0:T(8,128)(2,1)S(1)}, bf16[3200,128]{1,0:T(8,128)(2,1)}, u32[]{:S(2)}) copy-start(bf16[3200,128]{1,0:T(8,128)(2,1)} %get-tuple-element.22.inner_ref.refs_4_) | copy-start | bytes 2457604
  71.0 21.7 %copy-start.1 = (bf16[3200,128]{1,0:T(8,128)(2,1)S(1)}, bf16[3200,128]{1,0:T(8,128)(2,1)}, u32[]{:S(2)}) copy-start(bf16[3200,128]{1,0:T(8,128)(2,1)} %get-tuple-element.23.outer_ref.refs_5_) | copy-start | bytes 2457604
  86.0 38.3 %all-to-all-start.3 = ((bf16[64,40,128]{2,1,0:T(8,128)(2,1)}), bf16[64,40,128]{2,1,0:T(8,128)(2,1)S(1)}, u32[]{:S(2)}, u32[]{:S(2)}) async-start(bf16[64,40,128]{2,1,0:T(8,128)(2,1)} %shard_map.99), calls=%async_computation.3 | async-start | bytes 1310720 | tf_op jit(solution)/shard_map/all_to_all | solution.py:381
  92.1 10.5 %collective-permute-start.2 = (bf16[3200,128]{1,0:T(8,128)(2,1)S(1)}, bf16[3200,128]{1,0:T(8,128)(2,1)S(1)}, u32[]{:S(2)}, u32[]{:S(2)}) collective-permute-start(bf16[3200,128]{1,0:T(8,128)(2,1)S(1)} %copy-done.2), channel_id=1, source_target_pairs={{0,1},{1,0},{2,3},{3,2},{4,5},{5,4},{6,7},{7,6},{8,9},{9,8},{10,11... | collective-permute-start | bytes 2457608 | tf_op jit(solution)/shard_map/ppermute | solution.py:397
  92.6 26.0 %collective-permute-start.3 = (bf16[3200,128]{1,0:T(8,128)(2,1)S(1)}, bf16[3200,128]{1,0:T(8,128)(2,1)S(1)}, u32[]{:S(2)}, u32[]{:S(2)}) collective-permute-start(bf16[3200,128]{1,0:T(8,128)(2,1)S(1)} %copy-done.1), channel_id=1, source_target_pairs={{1,2},{3,4},{5,6},{7,8},{9,10},{11,12},{13,14},{15,16},{17,18},{19... | collective-permute-start | bytes 2457608 | tf_op jit(solution)/shard_map/ppermute | solution.py:397

commit v5 on v4

--- a/solution.py
+++ b/solution.py
@@ -145,7 +145,7 @@
     for part, lo in ((first, 0), (second, 6)):
         for copy in part:
             copy.wait()
-        lax.fori_loop(lo, lo + 6, conv, 0, unroll=2)
+        lax.fori_loop(lo, lo + 6, conv, 0, unroll=3)
     cot_copy.wait()
 
     def point(m, _):
@@ -197,9 +197,9 @@
 
     def rows(q, _):
         gs, xs = [], []
-        for y in range(4):
-            ystart = pl.multiple_of((4 * q + y) * CI, CI)
-            gstart = pl.multiple_of((4 * q + y + 1) * CO, CO)
+        for y in range(8):
+            ystart = pl.multiple_of((8 * q + y) * CI, CI)
+            gstart = pl.multiple_of((8 * q + y + 1) * CO, CO)
             for z, g in enumerate(gs_buf):
                 mid = g[pl.ds(gstart, CO), :]
                 wide = mid.astype(F32)
@@ -224,7 +224,7 @@
     for part, lo in ((first + g_first, 0), (second + g_second, 24)):
         for copy in part:
             copy.wait()
-        lax.fori_loop(lo // 4, lo // 4 + 6, rows, 0)
+        lax.fori_loop(lo // 8, lo // 8 + 3, rows, 0)
     out_ref[0:288, :] = acc[0:288, 0:128].astype(BF)
     side = acc[0:288, 128:192]
     tail = jnp.concatenate([side[160:288], jnp.zeros((32, CO), F32)], axis=0)

time: 128 us -> 125 us (0.977)
  Pallas kernels: 34.9 us -> 32.8 us
    pallas_call x1, Pallas kernels: 7.53 us -> 6.04 us  [layer(): taps = weight(*x, far(inner), far(outer))]
  transfers between devices with their start and end apart: 5 -> 5, of which waited for: 2 -> 2; matrix products, arithmetic and copies ran while one was open for 0% -> 0% of each run, Pallas kernels for 10% -> 11%
where the time goes in v5:
time: 125 us; the launch traced here: 123 us
  blocking collectives  48.7 us (39%)
  Pallas kernels  32.8 us (26%)
  waiting for transfers between devices  23.5 us (19%)
  starting transfers between devices  17.6 us (14%)
    all_to_all x3, blocking collectives, exchange(): return lax.all_to_all(parts, axes, 0, 0)  48.7 us
    ppermute x2, waiting for transfers between devices, swap(): lax.ppermute(outer, SPACE, off_chip)  23.4 us
    pallas_call x1, Pallas kernels, layer(): act, inner, outer = forward(*x, far(wf), bias, far(cotangent[0]))  9.36 us
    ppermute x2, starting transfers between devices, swap(): lax.ppermute(outer, SPACE, off_chip)  7.66 us
    all_to_all x1, starting transfers between devices, exchange(): return lax.all_to_all(parts, axes, 0, 0)  6.06 us
    pallas_call x1, Pallas kernels, layer(): taps = weight(*x, far(inner), far(outer))  6.04 us
    pallas_call x1, Pallas kernels, layer(): grad_volumes = finish(far(own0), far(own1), far_inner, far_outer, far(wb))  5.63 us
    pallas_call x1, Pallas kernels, layer(): own0, own1 = back(far(inner), far(outer), far(wb))  5.24 us
  transfers between devices with their start and end apart: 5, of which 2 were waited for; matrix products, arithmetic and copies ran while one was open for 0% of the time, Pallas kernels for 11%

profile of v5, /device:TPU:1, one launch (start us, length us, event | category | flops | bytes accessed | tf_op | source)
XLA Modules:
  0.0 123.3 jit_solution(12111007678454347288)
XLA Ops:
  0.6 0.0 copy-start
  0.6 2.2 %shard_map.92 = (bf16[1600,128]{1,0:T(8,128)(2,1)}, bf16[1600,128]{1,0:T(8,128)(2,1)}) custom-call(bf16[32,2,48,128]{3,2,1,0:T(8,128)(2,1)} %bitcast.14), custom_call_target="tpu_custom_call" | custom-call | flops 4194304 | bytes 3145728 | tf_op jit(solution)/shard_map/pallas_call | solution.py:491
  2.8 3.3 %collective-permute-start = (bf16[1600,128]{1,0:T(8,128)(2,1)}, bf16[1600,128]{1,0:T(8,128)(2,1)S(1)}, u32[]{:S(2)}, u32[]{:S(2)}) collective-permute-start(bf16[1600,128]{1,0:T(8,128)(2,1)} %get-tuple-element.18.refs_2_), channel_id=1, source_target_pairs={{0,1},{1,0},{2,3},{3,2},{4,5},{5,4},{6,7},{7,6},{8,9},{9,8},{10,11... | collective-permute-start | bytes 1228808 | tf_op jit(solution)/shard_map/ppermute | solution.py:397
  6.1 3.0 %collective-permute-start.1 = (bf16[1600,128]{1,0:T(8,128)(2,1)}, bf16[1600,128]{1,0:T(8,128)(2,1)S(1)}, u32[]{:S(2)}, u32[]{:S(2)}) collective-permute-start(bf16[1600,128]{1,0:T(8,128)(2,1)} %get-tuple-element.19.refs_3_), channel_id=1, source_target_pairs={{1,2},{3,4},{5,6},{7,8},{9,10},{11,12},{13,14},{15,16},{17,18},{19... | collective-permute-start | bytes 1228808 | tf_op jit(solution)/shard_map/ppermute | solution.py:397
  9.1 2.2 %shard_map.93 = (bf16[768,512]{1,0:T(8,128)(2,1)}, bf16[576,256]{1,0:T(8,128)(2,1)}, bf16[64,32,128]{2,1,0:T(8,128)(2,1)S(1)}) custom-call(bf16[3,3,3,32,64]{4,3,2,1,0:T(8,128)(2,1)} %bitcast.15, f32[2048,128]{1,0:T(8,128)} %bitcast.13), custom_call_target="tpu_custom_call" | custom-call | flops 4194304 | bytes 3145728 | tf_op jit(solution)/shard_map/pallas_call | solution.py:493
  11.3 0.0 collective-permute-done.refs_0_
  11.3 7.4 %collective-permute-done.1.refs_1_ = bf16[1600,128]{1,0:T(8,128)(2,1)S(1)} collective-permute-done((bf16[1600,128]{1,0:T(8,128)(2,1)}, bf16[1600,128]{1,0:T(8,128)(2,1)S(1)}, u32[]{:S(2)}, u32[]{:S(2)}) %collective-permute-start.1) | collective-permute-done | bytes 409632 | tf_op jit(solution)/shard_map/ppermute | solution.py:397
  18.7 0.0 copy-done
  18.7 9.4 %shard_map.94 = (bf16[64,2,48,128]{3,2,1,0:T(8,128)(2,1)}, bf16[3200,128]{1,0:T(8,128)(2,1)}, bf16[3200,128]{1,0:T(8,128)(2,1)}) custom-call(bf16[1600,128]{1,0:T(8,128)(2,1)S(1)} %collective-permute-done.refs_0_, bf16[1600,128]{1,0:T(8,128)(2,1)S(1)} %collective-permute-done.1.refs_1_, bf16[1600,128]{1,0:T(8,128)(2,1)} %get-tuple-element.18.refs_2_, ...), custom_call_target="tpu_custom_call" | custom-call | flops 12884901888 | bytes 8388608 | tf_op jit(solution)/shard_map/pallas_call | solution.py:496
  28.0 6.0 %shard_map.97 = bf16[512,128]{1,0:T(8,128)(2,1)S(1)} custom-call(bf16[1600,128]{1,0:T(8,128)(2,1)S(1)} %collective-permute-done.refs_0_, bf16[1600,128]{1,0:T(8,128)(2,1)S(1)} %collective-permute-done.1.refs_1_, bf16[1600,128]{1,0:T(8,128)(2,1)} %get-tuple-element.18.refs_2_, bf16[1600,128]{1,0:T(8,128)(2,1)} %get-tuple-element.19.refs_3_, ...), custom_call_target="tpu_custom_call" | custom-call | flops 12884901888 | bytes 5242880 | tf_op jit(solution)/shard_map/pallas_call | solution.py:498
  34.1 18.2 %all_to_all.20.t_ref = bf16[64,8,128]{2,1,0:T(8,128)(2,1)S(1)} all-to-all(bf16[64,8,128]{2,1,0:T(8,128)(2,1)S(1)} %bitcast.12), channel_id=1, replica_groups=mesh['yl'=2,'x'=4,'zh'=4,'zl'=2,'yh'=2,'c'=2] {'yl','x','zl','yh','c'}, dimensions={0} | all-to-all | bytes 262144 | tf_op jit(solution)/shard_map/all_to_all | solution.py:381
  52.3 16.5 %all_to_all.21.f_ref = bf16[64,32,128]{2,1,0:T(8,128)(2,1)S(1)} all-to-all(bf16[64,32,128]{2,1,0:T(8,128)(2,1)S(1)} %get-tuple-element.27), channel_id=1, replica_groups=mesh['yl'=2,'x'=4,'zh'=4,'zl'=2,'yh'=2,'c'=2] {'yl','x','zl','yh','c'}, dimensions={0} | all-to-all | bytes 1048576 | tf_op jit(solution)/shard_map/all_to_all | solution.py:381
  68.8 0.0 copy-start.2
  68.8 0.0 copy-start.1
  68.8 0.1 shard_map.98
  69.0 14.0 %all_to_all.22.in_ref = bf16[4,40,128]{2,1,0:T(8,128)(2,1)S(1)} all-to-all(bf16[4,40,128]{2,1,0:T(8,128)(2,1)S(1)} %shard_map.98), channel_id=1, replica_groups=mesh['yl'=2,'x'=4,'zh'=4,'zl'=2,'yh'=2,'c'=2] {'zh'}, dimensions={0} | all-to-all | bytes 81920 | tf_op jit(solution)/shard_map/all_to_all | solution.py:381
  82.9 0.9 shard_map.99
  83.8 6.1 %all-to-all-start.3 = ((bf16[64,40,128]{2,1,0:T(8,128)(2,1)}), bf16[64,40,128]{2,1,0:T(8,128)(2,1)S(1)}, u32[]{:S(2)}, u32[]{:S(2)}) async-start(bf16[64,40,128]{2,1,0:T(8,128)(2,1)} %shard_map.99), calls=%async_computation.3 | async-start | bytes 1310720 | tf_op jit(solution)/shard_map/all_to_all | solution.py:381
  89.9 0.0 copy-done.2
  89.9 0.6 collective-permute-start.2
  90.5 0.0 copy-done.1
  90.5 4.7 %collective-permute-start.3 = (bf16[3200,128]{1,0:T(8,128)(2,1)S(1)}, bf16[3200,128]{1,0:T(8,128)(2,1)S(1)}, u32[]{:S(2)}, u32[]{:S(2)}) collective-permute-start(bf16[3200,128]{1,0:T(8,128)(2,1)S(1)} %copy-done.1), channel_id=1, source_target_pairs={{1,2},{3,4},{5,6},{7,8},{9,10},{11,12},{13,14},{15,16},{17,18},{19... | collective-permute-start | bytes 2457608 | tf_op jit(solution)/shard_map/ppermute | solution.py:397
  95.1 5.2 %shard_map.95 = (f32[1536,128]{1,0:T(8,128)}, f32[1536,128]{1,0:T(8,128)}) custom-call(bf16[3200,128]{1,0:T(8,128)(2,1)} %get-tuple-element.22.inner_ref.refs_4_, bf16[3200,128]{1,0:T(8,128)(2,1)} %get-tuple-element.23.outer_ref.refs_5_, bf16[576,256]{1,0:T(8,128)(2,1)} %get-tuple-element.24.d_ref), custom_call_target="tpu_custom_call" | custom-call | flops 8589934592 | bytes 6291456 | tf_op jit(solution)/shard_map/pallas_call | solution.py:500
  100.4 0.0 collective-permute-done.2.inner_ref
  100.4 16.1 %collective-permute-done.3.outer_ref = bf16[3200,128]{1,0:T(8,128)(2,1)S(1)} collective-permute-done((bf16[3200,128]{1,0:T(8,128)(2,1)S(1)}, bf16[3200,128]{1,0:T(8,128)(2,1)S(1)}, u32[]{:S(2)}, u32[]{:S(2)}) %collective-permute-start.3) | collective-permute-done | bytes 819232 | tf_op jit(solution)/shard_map/ppermute | solution.py:397
  116.5 5.6 %shard_map.96 = bf16[32,2,48,128]{3,2,1,0:T(8,128)(2,1)} custom-call(f32[1536,128]{1,0:T(8,128)} %get-tuple-element.25.own0_ref, f32[1536,128]{1,0:T(8,128)} %get-tuple-element.26.own1_ref, bf16[3200,128]{1,0:T(8,128)(2,1)S(1)} %collective-permute-done.2.inner_ref, bf16[3200,128]{1,0:T(8,128)(2,1)S(1)} %collective-permute-done.3.outer_ref, ...), custom_call_target="tpu_custom_call" | custom-call | flops 4294967296 | bytes 6291456 | tf_op jit(solution)/shard_map/pallas_call | solution.py:505
  122.1 0.0 all-to-all-done.3.in_ref
  122.1 1.2 shard_map.100
Async XLA Ops:
  0.6 18.0 %copy-start = (f32[64]{0:T(128)S(1)}, f32[64]{0:T(128)}, u32[]{:S(2)}) copy-start(f32[64]{0:T(128)} %refs_5_.1) | copy-start | bytes 772
  2.8 8.5 %collective-permute-start = (bf16[1600,128]{1,0:T(8,128)(2,1)}, bf16[1600,128]{1,0:T(8,128)(2,1)S(1)}, u32[]{:S(2)}, u32[]{:S(2)}) collective-permute-start(bf16[1600,128]{1,0:T(8,128)(2,1)} %get-tuple-element.18.refs_2_), channel_id=1, source_target_pairs={{0,1},{1,0},{2,3},{3,2},{4,5},{5,4},{6,7},{7,6},{8,9},{9,8},{10,11... | collective-permute-start | bytes 1228808 | tf_op jit(solution)/shard_map/ppermute | solution.py:397
  6.1 12.6 %collective-permute-start.1 = (bf16[1600,128]{1,0:T(8,128)(2,1)}, bf16[1600,128]{1,0:T(8,128)(2,1)S(1)}, u32[]{:S(2)}, u32[]{:S(2)}) collective-permute-start(bf16[1600,128]{1,0:T(8,128)(2,1)} %get-tuple-element.19.refs_3_), channel_id=1, source_target_pairs={{1,2},{3,4},{5,6},{7,8},{9,10},{11,12},{13,14},{15,16},{17,18},{19... | collective-permute-start | bytes 1228808 | tf_op jit(solution)/shard_map/ppermute | solution.py:397
  68.8 21.1 %copy-start.2 = (bf16[3200,128]{1,0:T(8,128)(2,1)S(1)}, bf16[3200,128]{1,0:T(8,128)(2,1)}, u32[]{:S(2)}) copy-start(bf16[3200,128]{1,0:T(8,128)(2,1)} %get-tuple-element.22.inner_ref.refs_4_) | copy-start | bytes 2457604
  68.8 21.6 %copy-start.1 = (bf16[3200,128]{1,0:T(8,128)(2,1)S(1)}, bf16[3200,128]{1,0:T(8,128)(2,1)}, u32[]{:S(2)}) copy-start(bf16[3200,128]{1,0:T(8,128)(2,1)} %get-tuple-element.23.outer_ref.refs_5_) | copy-start | bytes 2457604
  83.8 38.3 %all-to-all-start.3 = ((bf16[64,40,128]{2,1,0:T(8,128)(2,1)}), bf16[64,40,128]{2,1,0:T(8,128)(2,1)S(1)}, u32[]{:S(2)}, u32[]{:S(2)}) async-start(bf16[64,40,128]{2,1,0:T(8,128)(2,1)} %shard_map.99), calls=%async_computation.3 | async-start | bytes 1310720 | tf_op jit(solution)/shard_map/all_to_all | solution.py:381
  89.9 10.5 %collective-permute-start.2 = (bf16[3200,128]{1,0:T(8,128)(2,1)S(1)}, bf16[3200,128]{1,0:T(8,128)(2,1)S(1)}, u32[]{:S(2)}, u32[]{:S(2)}) collective-permute-start(bf16[3200,128]{1,0:T(8,128)(2,1)S(1)} %copy-done.2), channel_id=1, source_target_pairs={{0,1},{1,0},{2,3},{3,2},{4,5},{5,4},{6,7},{7,6},{8,9},{9,8},{10,11... | collective-permute-start | bytes 2457608 | tf_op jit(solution)/shard_map/ppermute | solution.py:397
  90.5 26.0 %collective-permute-start.3 = (bf16[3200,128]{1,0:T(8,128)(2,1)S(1)}, bf16[3200,128]{1,0:T(8,128)(2,1)S(1)}, u32[]{:S(2)}, u32[]{:S(2)}) collective-permute-start(bf16[3200,128]{1,0:T(8,128)(2,1)S(1)} %copy-done.1), channel_id=1, source_target_pairs={{1,2},{3,4},{5,6},{7,8},{9,10},{11,12},{13,14},{15,16},{17,18},{19... | collective-permute-start | bytes 2457608 | tf_op jit(solution)/shard_map/ppermute | solution.py:397
